TPU v7x, 32 devices: a whole 2x2x4 slice. The times are simulated.
32 devices in a mesh: gx: 8 (over y, x, core), gy: 4 (over z).
Axes of the slice: x: 2, y: 2, z: 4, core: 2. Of those that a mesh axis runs over, the one named last changes fastest.
Arguments:
- right_side: float32 [2, 128, 512], P(None, 'gx', 'gy'), may hold values from -160 to 160
- conductivity: float32 [128, 512], P('gx', 'gy'), may hold values from 0.2 to 5
- leaf_inverse: float32 [32, 16, 128, 128], P('gx', 'gy'), may hold values from -1 to 4, as said below
- front_basis: float32 [128, 512, 128], P('gx', 'gy'), may hold values from -0.25 to 0.25
- leaf_transfer: float32 [8, 4, 128, 128], P('gx', 'gy'), may hold values from -0.4375 to 0.4375
- node_transfer: float32 [8, 4, 4, 128, 128], P('gx', 'gy'), may hold values from -1 to 1, as said below
- leaf_front: float32 [8, 4, 128, 128], P('gx', 'gy'), may hold values from -1 to 1, as said below
- node_front: float32 [8, 4, 5, 128, 128], P('gx', 'gy'), may hold values from -1 to 1, as said below
Outputs:
- solution: float32 [2, 128, 512], P(None, 'gx', 'gy')
- residual: float32 [2, 128, 512], P(None, 'gx', 'gy')
- direction: float32 [2, 128, 512], P(None, 'gx', 'gy')
Inputs may be any that keep to these rules, and one draw needn't show every extreme that they name: `leaf_inverse`: every block is symmetric and positive definite. `leaf_front`: every matrix is symmetric and positive definite. `node_front`: every matrix is symmetric and positive definite; entry h - 1 is the same for all tiles covered by one node of level h. `node_transfer`: entry h - 1 is the same for all tiles covered by one node of level h.
All inputs are finite; a program needn't handle non-finite values.
Results may differ from a plain program's by a relative error of at most 0.0001.
Values sent between devices are 32-bit elements; how exact they have to be, the bound alone decides.
No kernel may reach another device: no remote copies, remote signals or barrier semaphores. Data moves between devices by JAX's collectives and lax.ppermute only.
A program may use at most 64 MiB of HBM per device.

v0:
```python
import jax
import jax.numpy as jnp
from jax import lax
from jax.experimental import pallas as pl
from jax.experimental.pallas import tpu as pltpu
from jax.sharding import PartitionSpec as P

LBX = 4
LBY = 32
AXES = ("gx", "gy")
F32 = jnp.float32
BF16 = jnp.bfloat16
VMEM_LIMIT = 12 << 20
PIECES = 4


ROWS = (((1,), (0,)), ((), ()))
LANES = (((1,), (1,)), ((), ()))


def parts(value):
    high = value.astype(BF16)
    return high, (value - high.astype(F32)).astype(BF16)


def stacked(rows):
    high = rows.astype(BF16).astype(F32)
    rest = rows - high
    middle = rest.astype(BF16).astype(F32)
    return jnp.concatenate([high, middle, rest - middle], axis=0).astype(BF16)


def rows_times(rows, high, low, dims=ROWS):
    split = stacked(rows)
    count = rows.shape[0]
    total = lax.dot_general(split, low, dims, preferred_element_type=F32)
    total = total + lax.dot_general(split, high, dims, preferred_element_type=F32)
    return total[:count] + (total[count : 2 * count] + total[2 * count :])


def product(a, b):
    high, low = parts(b)
    left = jnp.concatenate(parts(a), axis=0)
    count = a.shape[0]
    total = lax.dot_general(left, low, ROWS, preferred_element_type=F32)
    total = total + lax.dot_general(left, high, ROWS, preferred_element_type=F32)
    return total[:count] + total[count:]


def in_vmem(*shape, dtype=F32):
    return pltpu.VMEM(shape, dtype)


def in_hbm(*shape, dtype=F32):
    return pltpu.HBM(shape, dtype)


def call(body, outs, arrays, flops, scratch=(), fetched=(), written=False):
    vmem = pl.BlockSpec(memory_space=pltpu.VMEM)
    hbm = pl.BlockSpec(memory_space=pltpu.HBM)
    size = sum(a.size * a.dtype.itemsize for a in arrays)
    fetched = [pltpu.with_memory_space_constraint(a, pltpu.HBM) for a in fetched]
    return pl.pallas_call(
        body,
        out_shape=tuple(outs),
        in_specs=[hbm] * len(fetched) + [vmem] * len(arrays),
        out_specs=(hbm if written else vmem,) * len(outs),
        scratch_shapes=scratch,
        compiler_params=pltpu.CompilerParams(vmem_limit_bytes=VMEM_LIMIT),
        cost_estimate=pl.CostEstimate(flops=flops, bytes_accessed=size, transcendentals=0),
    )(*fetched, *arrays)


def place():
    return lax.axis_index("gx") * lax.axis_size("gy") + lax.axis_index("gy")


def odd(axis):
    return lax.rem(lax.axis_index(axis), 2) == 1


def cousins(me, level):
    return ((me >> (level - 1)) ^ 1) << (level - 1)


def flat(ref):
    return jnp.concatenate([ref[:, x, :] for x in range(ref.shape[1])], axis=1)


def send_rows(sent, chain):
    me = place()
    count_s = chain[0].shape[0]
    for level in range(1, len(chain) + 1):
        size = 1 << (level - 1)
        rows = jnp.broadcast_to(chain[level - 1][None], (size,) + chain[level - 1].shape)
        sent[pl.ds(cousins(me, level), size), 0:count_s, :] = rows
    sent[me, 0:count_s, :] = jnp.zeros(chain[0].shape, F32)


def project_kernel(
    leaf_t, node_t, values_hbm, basis_hbm, conduct_hbm,
    sent, own, wide_high, wide_low, up_high, up_low, moves, values, conduct, basis, sems,
):
    levels, rank = moves.shape[0], moves.shape[1]
    piece = basis.shape[0] // PIECES
    pairs = [(values_hbm, values), (leaf_t, moves.at[0]), (node_t, moves.at[pl.ds(1, levels - 1)])]
    pairs += [(basis_hbm.at[pl.ds(i * piece, piece)], basis.at[pl.ds(i * piece, piece)]) for i in range(PIECES)]
    pairs += [(conduct_hbm, conduct)]
    copies = [pltpu.make_async_copy(source, target, sems.at[i]) for i, (source, target) in enumerate(pairs)]
    for copy in copies:
        copy.start()
    for copy in copies[:3]:
        copy.wait()
    rows = flat(values)
    coeffs = jnp.zeros(own.shape, F32)
    up = moves[0]
    up_high[:, 0:rank], up_low[:, 0:rank] = parts(up)
    for i in range(max(PIECES, levels - 1)):
        if i < PIECES:
            copies[3 + i].wait()
            at = slice(i * piece, (i + 1) * piece)
            held = basis[at, :]
            coeffs = coeffs + rows_times(rows[:, at], *parts(held))
            wide_high[:, at], wide_low[:, at] = parts(held.T)
        if i + 1 < levels:
            up = product(up, moves[i + 1])
            at = slice((i + 1) * rank, (i + 2) * rank)
            up_high[:, at], up_low[:, at] = parts(up)
    own[...] = coeffs
    send_chain(sent, coeffs, up_high, up_low)
    copies[3 + PIECES].wait()


def send_chain(sent, coeffs, up_high, up_low):
    rank = coeffs.shape[1]
    chain = rows_times(coeffs, up_high[...], up_low[...])
    send_rows(sent, [chain[:, i : i + rank] for i in range(0, chain.shape[1], rank)])


def window_kernel(
    leaf_f, node_f, inverse_hbm, values, moves, up_high, up_low,
    near, down_high, down_low, inverse, fronts, held, sems,
):
    levels, rank = moves.shape[0], moves.shape[1]
    copies = [
        pltpu.make_async_copy(leaf_f, fronts.at[0], sems.at[0]),
        pltpu.make_async_copy(node_f, fronts.at[pl.ds(1, levels)], sems.at[1]),
        pltpu.make_async_copy(inverse_hbm, inverse, sems.at[2]),
    ]
    for copy in copies:
        copy.start()
    columns = [slice(h * rank, (h + 1) * rank) for h in range(levels + 1)]
    back = [(up_high[:, at].astype(F32) + up_low[:, at].astype(F32)).T for at in columns[:levels]]
    copies[0].wait()
    copies[1].wait()
    total = [fronts[0]] + [product(fronts[h + 1], back[h]) for h in range(levels)]
    copies[2].wait()
    for h in range(levels, -1, -1):
        if h < levels:
            total[h] = total[h] + product(moves[h], total[h + 1])
        down_high[columns[h], :], down_low[columns[h], :] = parts(total[h])
    leaf_map(values, inverse, near, held)


def tree(got, own, down_high, down_low):
    me = place()
    count_s, rank = own.shape
    rows = [own[...]]
    for level in range(1, down_high.shape[0] // rank):
        size = 1 << (level - 1)
        rows.append(jnp.sum(got[pl.ds(cousins(me, level), size), 0:count_s, :], axis=0))
    return rows_times(jnp.concatenate(rows, axis=1), down_high[...], down_low[...])


def expand_into(out, spread, wide_high, wide_low, near):
    far = rows_times(spread, wide_high[...], wide_low[...])
    width = out.shape[2]
    for x in range(out.shape[1]):
        out[:, x, :] = near[:, x, :] + far[:, x * width : (x + 1) * width]


def edge_column(values, conduct, at):
    lane = lax.broadcasted_iota(jnp.int32, conduct.shape, 1)
    column = jnp.broadcast_to(conduct[:, at : at + 1], conduct.shape)
    for s in range(values.shape[0]):
        column = jnp.where(lane == s, jnp.broadcast_to(values[s, :, at : at + 1], conduct.shape), column)
    return column


def first_kernel(
    got, own, down_high, down_low, wide_high, wide_low, near, right, conduct,
    z, x_inner, x_outer, y_inner, y_outer, sums,
):
    expand_into(z, tree(got, own, down_high, down_low), wide_high, wide_low, near)
    count_s, extent_x, extent_y = z.shape
    odd_x, odd_y = odd("gx"), odd("gy")
    for s in range(count_s):
        head, tail = z[s, 0:1, :], z[s, extent_x - 1 : extent_x, :]
        x_inner[s : s + 1, :] = jnp.where(odd_x, head, tail)
        x_outer[s : s + 1, :] = jnp.where(odd_x, tail, head)
    head, tail = conduct[0:1, :], conduct[extent_x - 1 : extent_x, :]
    x_inner[count_s : count_s + 1, :] = jnp.where(odd_x, head, tail)
    x_outer[count_s : count_s + 1, :] = jnp.where(odd_x, tail, head)
    values, cond = z[...], conduct[...]
    head, tail = edge_column(values, cond, 0), edge_column(values, cond, extent_y - 1)
    y_inner[...] = jnp.where(odd_y, head, tail)
    y_outer[...] = jnp.where(odd_y, tail, head)
    sums[...] = jnp.sum(right[...] * values, axis=(1, 2))[:, None] * jnp.ones((1, extent_y), F32)


def second_kernel(
    x_inner, x_outer, y_inner, y_outer, z, conduct, wide_high, wide_low, sums, up_high, up_low, inverse,
    applied, near, sent, own, held,
):
    count_s, extent_x, extent_y = z.shape
    odd_x, odd_y = odd("gx"), odd("gy")
    above = jnp.where(odd_x, x_inner[...], x_outer[...])
    below = jnp.where(odd_x, x_outer[...], x_inner[...])
    before = jnp.where(odd_y, y_inner[...], y_outer[...])
    after = jnp.where(odd_y, y_outer[...], y_inner[...])
    shape = (extent_x, extent_y)
    row = lax.broadcasted_iota(jnp.int32, shape, 0)
    lane = lax.broadcasted_iota(jnp.int32, shape, 1)

    def beside(field, at):
        down = jnp.where(row == extent_x - 1, below[at : at + 1, :], pltpu.roll(field, extent_x - 1, 0))
        up = jnp.where(row == 0, above[at : at + 1, :], pltpu.roll(field, 1, 0))
        right = jnp.where(lane == extent_y - 1, after[:, at : at + 1], pltpu.roll(field, extent_y - 1, 1))
        left = jnp.where(lane == 0, before[:, at : at + 1], pltpu.roll(field, 1, 1))
        return down, up, right, left

    cond = conduct[...]
    weights = [0.5 * (cond + other) for other in beside(cond, count_s)]
    lanes = lax.broadcasted_iota(jnp.int32, (1, extent_y), 1)
    packed = []
    for s in range(count_s):
        values = z[s]
        total = jnp.zeros(shape, F32)
        for weight, other in zip(weights, beside(values, s)):
            total = total + weight * (values - other)
        applied[s] = total
        curvature = jnp.sum(values * total)
        packed.append(jnp.where(lanes == 0, sums[s : s + 1, :], jnp.where(lanes == 1, curvature, 0.0)))
    coeffs = rows_times(flat(applied), wide_high[...], wide_low[...], LANES)
    own[...] = coeffs
    send_chain(sent, coeffs, up_high, up_low)
    scalars = jnp.concatenate(packed, axis=0)
    sent[:, count_s:, :] = jnp.broadcast_to(scalars[None], (sent.shape[0],) + scalars.shape)
    leaf_map(applied, inverse, near, held)


def third_kernel(
    got, own, down_high, down_low, wide_high, wide_low, near, z, right, applied,
    sent, totals, solution, residual, partial_d, far,
):
    count_s = own.shape[0]
    spread = tree(got, own, down_high, down_low)
    scalars = jnp.sum(got[:, count_s:, :], axis=0)
    totals[...] = scalars
    square = jnp.sum(near[...] * applied[...], axis=(1, 2)) + jnp.sum(own[...] * spread, axis=1)
    lanes = lax.broadcasted_iota(jnp.int32, (1, sent.shape[1]), 1)
    row = jnp.zeros((1, sent.shape[1]), F32)
    for s in range(count_s):
        row = jnp.where(lanes == s, square[s], row)
    sent[...] = jnp.broadcast_to(row, sent.shape)
    expand_into(far, spread, wide_high, wide_low, near)
    for s in range(count_s):
        step = scalars[s : s + 1, 0:1] / scalars[s : s + 1, 1:2]
        solution[s] = step * z[s]
        residual[s] = right[s] - step * applied[s]
        partial_d[s] = z[s] - step * far[s]


def last_kernel(got, totals, z, partial_d, solution, residual, solution_hbm, residual_hbm, direction_hbm, direction, sems):
    copies = [
        pltpu.make_async_copy(solution, solution_hbm, sems.at[0]),
        pltpu.make_async_copy(residual, residual_hbm, sems.at[1]),
        pltpu.make_async_copy(direction, direction_hbm, sems.at[2]),
    ]
    copies[0].start()
    copies[1].start()
    square = jnp.sum(got[...], axis=0, keepdims=True)
    for s in range(z.shape[0]):
        curvature = totals[s : s + 1, 1:2]
        step = totals[s : s + 1, 0:1] / curvature
        ratio = step * square[0:1, s : s + 1] / curvature - 1.0
        direction[s] = partial_d[s] + ratio * z[s]
    copies[2].start()
    for copy in copies:
        copy.wait()


def leaf_map(values, inverse, out, held):
    count_s, extent_x, extent_y = values.shape
    blocks_x = extent_x // LBX
    rows = count_s * blocks_x
    group = lax.broadcasted_iota(jnp.int32, (rows, extent_y), 1) // LBY
    owner = lax.rem(lax.broadcasted_iota(jnp.int32, (rows, extent_y), 0), blocks_x)

    def regroup(lines):
        outs = []
        for q in range(len(lines)):
            out_q = lines[q]
            for a in range(len(lines)):
                if a != q:
                    turned = pltpu.roll(lines[a], ((a - q) * LBY) % extent_y, 1)
                    out_q = jnp.where(group == a, turned, out_q)
            outs.append(out_q)
        return outs

    lines = [
        jnp.concatenate(
            [values[s, p * LBX + a : p * LBX + a + 1, :] for s in range(count_s) for p in range(blocks_x)], axis=0
        )
        for a in range(LBX)
    ]
    mapped = []
    for q, block in enumerate(regroup(lines)):
        wide = jnp.concatenate([jnp.where(owner == p, block, 0.0) for p in range(blocks_x)], axis=1)
        stack = jnp.concatenate([inverse[p, q] for p in range(blocks_x)], axis=0)
        mapped.append(rows_times(wide, *parts(stack)))
    for a, line in enumerate(regroup(mapped)):
        held[a] = line
    for s in range(count_s):
        for p in range(blocks_x):
            for a in range(LBX):
                out[s, p * LBX + a : p * LBX + a + 1, :] = held[a, s * blocks_x + p : s * blocks_x + p + 1, :]


def pair_exchange(inner_value, outer_value, axis):
    count = lax.axis_size(axis)
    inner = [(i, i ^ 1) for i in range(count)]
    outer = []
    for i in range(1, count - 1, 2):
        outer += [(i, i + 1), (i + 1, i)]
    inner_value = lax.ppermute(inner_value, axis, inner)
    outer_value = lax.ppermute(outer_value, axis, outer)
    return inner_value, outer_value


def on_device(
    right_side,
    conductivity,
    leaf_inverse,
    front_basis,
    leaf_transfer,
    node_transfer,
    leaf_front,
    node_front,
):
    levels = node_front.shape[2]
    count = 1 << levels
    count_s, extent_x, extent_y = right_side.shape
    rank = front_basis.shape[-1]
    basis = front_basis.reshape(extent_x * extent_y, rank)
    leaf_t, node_t = leaf_transfer[0, 0], node_transfer[0, 0]
    leaf_f, node_f = leaf_front[0, 0], node_front[0, 0]
    field = (count_s, extent_x, extent_y)
    cells = extent_x * extent_y

    def pair(*shape):
        return (in_vmem(*shape, dtype=BF16),) * 2

    sent, own, wide_high, wide_low, up_high, up_low, moves, right_side, conductivity = call(
        project_kernel,
        (
            in_hbm(count, count_s, rank),
            in_vmem(count_s, rank),
            *pair(rank, cells),
            *pair(rank, levels * rank),
            in_vmem(levels, rank, rank),
            in_vmem(*field),
            in_vmem(extent_x, extent_y),
        ),
        (),
        10**6,
        (pltpu.VMEM((cells, rank), F32), pltpu.SemaphoreType.DMA((4 + PIECES,))),
        (leaf_t, node_t, right_side, basis, conductivity),
    )
    got = lax.all_to_all(sent, AXES, 0, 0)
    held = pltpu.VMEM((LBX, count_s * extent_x // LBX, extent_y), F32)
    near, down_high, down_low, inverse = call(
        window_kernel,
        (in_vmem(*field), *pair((levels + 1) * rank, rank), in_vmem(*leaf_inverse.shape)),
        (right_side, moves, up_high, up_low),
        10**7,
        (pltpu.VMEM((levels + 1, rank, rank), F32), held, pltpu.SemaphoreType.DMA((3,))),
        (leaf_f, node_f, leaf_inverse),
    )
    edge = (count_s + 1, extent_y)
    first_z, x_inner, x_outer, y_inner, y_outer, sums = call(
        first_kernel,
        [in_vmem(*s) for s in (field, edge, edge, (extent_x, extent_y), (extent_x, extent_y), (count_s, extent_y))],
        (got, own, down_high, down_low, wide_high, wide_low, near, right_side, conductivity),
        10**6,
    )
    x_inner, x_outer = pair_exchange(x_inner, x_outer, "gx")
    y_inner, y_outer = pair_exchange(y_inner, y_outer, "gy")
    applied, near, sent, own = call(
        second_kernel,
        (in_vmem(*field), in_vmem(*field), in_vmem(count, 2 * count_s, rank), in_vmem(count_s, rank)),
        (x_inner, x_outer, y_inner, y_outer, first_z, conductivity, wide_high, wide_low, sums, up_high, up_low, inverse),
        10**6,
        (held,),
    )
    got = lax.all_to_all(sent, AXES, 0, 0)
    sent, totals, step_z, residual, partial_d = call(
        third_kernel,
        (in_vmem(count, rank), in_vmem(count_s, rank), in_vmem(*field), in_vmem(*field), in_vmem(*field)),
        (got, own, down_high, down_low, wide_high, wide_low, near, first_z, right_side, applied),
        10**6,
        (pltpu.VMEM(field, F32),),
    )
    got = lax.all_to_all(sent, AXES, 0, 0, tiled=True)
    return call(
        last_kernel,
        (in_hbm(*field),) * 3,
        (got, totals, first_z, partial_d, step_z, residual),
        10**6,
        (pltpu.VMEM(field, F32), pltpu.SemaphoreType.DMA((3,))),
        written=True,
    )


def solution(mesh):
    return jax.shard_map(
        on_device,
        mesh=mesh,
        in_specs=(
            P(None, "gx", "gy"),
            P("gx", "gy"),
            P("gx", "gy", None, None),
            P("gx", "gy", None),
            P("gx", "gy", None, None),
            P("gx", "gy", None, None, None),
            P("gx", "gy", None, None),
            P("gx", "gy", None, None, None),
        ),
        out_specs=(P(None, "gx", "gy"), P(None, "gx", "gy"), P(None, "gx", "gy")),
        check_vma=False,
    )
```

profile of v0, /device:TPU:0, one launch (start us, length us, event | category | flops | bytes accessed | tf_op | source)
XLA Modules:
  0.0 49.2 jit_solution(11352043068510942539)
XLA Ops:
  0.6 2.8 %shard_map.103 = (f32[32,2,128]{2,1,0:T(2,128)}, f32[2,128]{1,0:T(2,128)S(1)}, bf16[128,2048]{1,0:T(8,128)(2,1)S(1)}, bf16[128,2048]{1,0:T(8,128)(2,1)S(1)}, bf1...) custom-call(f32[128,128]{1,0:T(8,128)} %bitcast.14, ...), custom_call_target="tpu_custom_call" | custom-call | flops 1000000 | tf_op jit(solution)/shard_map/pallas_call | solution.py:63
  3.5 7.3 %all-to-all-start = ((f32[32,2,128]{2,1,0:T(2,128)}), f32[32,2,128]{2,1,0:T(2,128)S(1)}, u32[]{:S(2)}, u32[]{:S(2)}) async-start(f32[32,2,128]{2,1,0:T(2,128)} %get-tuple-element.31), calls=%async_computation | async-start | bytes 65536 | tf_op jit(solution)/shard_map/all_to_all | solution.py:380
  10.8 2.6 %shard_map.104 = (f32[2,16,128]{2,1,0:T(8,128)S(1)}, bf16[768,128]{1,0:T(8,128)(2,1)S(1)}, bf16[768,128]{1,0:T(8,128)(2,1)S(1)}, f32[4,4,128,128]{3,2,1,0:T(8,128)S(1)}) custom-call(f32[128,128]{1,0:T(8,128)} %bitcast.15, f32[5,128,128]{2,1,0:T(8,128)} %bitcast.12, f32[4,4,128,128]{3,2,1,0:T(8,128)} %inverse_hbm.1, ...), custom_call_target="tpu_custom_call" | custom-call | flops 10000000 | bytes 671744 | tf_op jit(solution)/shard_map/pallas_call | solution.py:63
  13.4 4.7 %all-to-all-done.got = f32[32,2,128]{2,1,0:T(2,128)S(1)} async-done(((f32[32,2,128]{2,1,0:T(2,128)}), f32[32,2,128]{2,1,0:T(2,128)S(1)}, u32[]{:S(2)}, u32[]{:S(2)}) %all-to-all-start) | async-done | bytes 32800 | tf_op jit(solution)/shard_map/all_to_all | solution.py:380
  18.1 0.5 %shard_map.105 = (f32[2,16,128]{2,1,0:T(8,128)S(1)}, f32[3,128]{1,0:T(4,128)S(1)}, f32[3,128]{1,0:T(4,128)S(1)}, f32[16,128]{1,0:T(8,128)S(1)}, f32[16,128]{1,0:T(8,128)S(1)}, /*index=5*/f32[2,128]{1,0:T(2,128)S(1)}) custom-call(f32[32,2,128]{2,1,0:T(2,128)S(1)} %all-to-all-done.got, f32[2,128]{1,0:T(2,128)S(1)} %get-tuple-element.32.own, ...), custom_call_target="tpu_custom_call" | custom-call | flops 1000000 | bytes 1516544 | tf_op jit(solution)/shard_map/pallas_call | solution.py:63
  18.7 0.5 collective-permute-start.2
  19.1 0.6 %collective-permute-start.3 = (f32[16,128]{1,0:T(8,128)S(1)}, f32[16,128]{1,0:T(8,128)S(1)}, u32[]{:S(2)}, u32[]{:S(2)}) collective-permute-start(f32[16,128]{1,0:T(8,128)S(1)} %get-tuple-element.46), channel_id=1, source_target_pairs={{1,2},{2,1},{5,6},{6,5},{9,10},{10,9},{13,14},{14,13},{17,18},{18,... | collective-permute-start | bytes 24584 | tf_op jit(solution)/shard_map/ppermute | solution.py:337
  19.8 0.1 collective-permute-start
  19.9 0.7 %collective-permute-start.1 = (f32[3,128]{1,0:T(4,128)S(1)}, f32[3,128]{1,0:T(4,128)S(1)}, u32[]{:S(2)}, u32[]{:S(2)}) collective-permute-start(f32[3,128]{1,0:T(4,128)S(1)} %get-tuple-element.44), channel_id=1, source_target_pairs={{4,8},{8,4},{12,16},{16,12},{20,24},{24,20},{5,9},{9,5},{13,17},{1... | collective-permute-start | bytes 4616 | tf_op jit(solution)/shard_map/ppermute | solution.py:337
  20.5 0.5 collective-permute-done.x_inner
  21.0 0.0 collective-permute-done.1.x_outer
  21.0 1.4 %collective-permute-done.2.y_inner = f32[16,128]{1,0:T(8,128)S(1)} collective-permute-done((f32[16,128]{1,0:T(8,128)S(1)}, f32[16,128]{1,0:T(8,128)S(1)}, u32[]{:S(2)}, u32[]{:S(2)}) %collective-permute-start.2) | collective-permute-done | bytes 8224 | tf_op jit(solution)/shard_map/ppermute | solution.py:336
  22.4 0.0 collective-permute-done.3.y_outer
  22.4 1.2 %shard_map.106 = (f32[2,16,128]{2,1,0:T(8,128)S(1)}, f32[2,16,128]{2,1,0:T(8,128)S(1)}, f32[32,4,128]{2,1,0:T(4,128)S(1)}, f32[2,128]{1,0:T(2,128)S(1)}) custom-call(f32[3,128]{1,0:T(4,128)S(1)} %collective-permute-done.x_inner, f32[3,128]{1,0:T(4,128)S(1)} %collective-permute-done.1.x_outer, f32[16,128]{1,0:T(8,128)S(1)} %collective-permute-done.2.y_inner, ...), custom_call_target="tpu_custom_call" | custom-call | flops 1000000 | bytes 2469888 | tf_op jit(solution)/shard_map/pallas_call | solution.py:63
  23.6 15.4 %all_to_all.21.got = f32[32,4,128]{2,1,0:T(4,128)S(1)} all-to-all(f32[32,4,128]{2,1,0:T(4,128)S(1)} %get-tuple-element.50), channel_id=1, replica_groups=mesh['gx'=8,'gy'=4] {'gx','gy'}, dimensions={0} | all-to-all | bytes 131072 | tf_op jit(solution)/shard_map/all_to_all | solution.py:406
  39.1 0.5 shard_map.107
  39.5 8.9 %all_to_all.22 = f32[32,1,128]{2,1,0:T(1,128)S(1)} all-to-all(f32[32,1,128]{2,1,0:T(1,128)S(1)} %bitcast.10), channel_id=1, replica_groups=mesh['gx'=8,'gy'=4] {'gx','gy'}, dimensions={0} | all-to-all | bytes 32768 | tf_op jit(solution)/shard_map/all_to_all | solution.py:414
  48.4 0.7 %shard_map.108 = (f32[2,16,128]{2,1,0:T(8,128)}, f32[2,16,128]{2,1,0:T(8,128)}, f32[2,16,128]{2,1,0:T(8,128)}) custom-call(f32[32,128]{1,0:T(8,128)S(1)} %bitcast.9, f32[2,128]{1,0:T(2,128)S(1)} %get-tuple-element.55.totals, f32[2,16,128]{2,1,0:T(8,128)S(1)} %get-tuple-element.47.z, f32[2,16,128]{2,1,0:T(8,128)S(1)} %get-tuple-element.56.partial_d, ...), custom_call_target="tpu_custom_call" | custom-call | flops 1000000 | bytes 82944 | tf_op jit(solution)/shard_map/pallas_call | solution.py:63
Async XLA Ops:
  3.5 14.6 %all-to-all-start = ((f32[32,2,128]{2,1,0:T(2,128)}), f32[32,2,128]{2,1,0:T(2,128)S(1)}, u32[]{:S(2)}, u32[]{:S(2)}) async-start(f32[32,2,128]{2,1,0:T(2,128)} %get-tuple-element.31), calls=%async_computation | async-start | bytes 65536 | tf_op jit(solution)/shard_map/all_to_all | solution.py:380
  18.7 3.7 %collective-permute-start.2 = (f32[16,128]{1,0:T(8,128)S(1)}, f32[16,128]{1,0:T(8,128)S(1)}, u32[]{:S(2)}, u32[]{:S(2)}) collective-permute-start(f32[16,128]{1,0:T(8,128)S(1)} %get-tuple-element.45), channel_id=1, source_target_pairs={{0,1},{1,0},{2,3},{3,2},{4,5},{5,4},{6,7},{7,6},{8,9},{9,8},{10,11... | collective-permute-start | bytes 24584 | tf_op jit(solution)/shard_map/ppermute | solution.py:336
  19.1 3.3 %collective-permute-start.3 = (f32[16,128]{1,0:T(8,128)S(1)}, f32[16,128]{1,0:T(8,128)S(1)}, u32[]{:S(2)}, u32[]{:S(2)}) collective-permute-start(f32[16,128]{1,0:T(8,128)S(1)} %get-tuple-element.46), channel_id=1, source_target_pairs={{1,2},{2,1},{5,6},{6,5},{9,10},{10,9},{13,14},{14,13},{17,18},{18,... | collective-permute-start | bytes 24584 | tf_op jit(solution)/shard_map/ppermute | solution.py:337
  19.8 1.2 %collective-permute-start = (f32[3,128]{1,0:T(4,128)S(1)}, f32[3,128]{1,0:T(4,128)S(1)}, u32[]{:S(2)}, u32[]{:S(2)}) collective-permute-start(f32[3,128]{1,0:T(4,128)S(1)} %get-tuple-element.43), channel_id=1, source_target_pairs={{0,4},{4,0},{8,12},{12,8},{16,20},{20,16},{24,28},{28,24},{1,5},{5... | collective-permute-start | bytes 4616 | tf_op jit(solution)/shard_map/ppermute | solution.py:336
  19.9 1.2 %collective-permute-start.1 = (f32[3,128]{1,0:T(4,128)S(1)}, f32[3,128]{1,0:T(4,128)S(1)}, u32[]{:S(2)}, u32[]{:S(2)}) collective-permute-start(f32[3,128]{1,0:T(4,128)S(1)} %get-tuple-element.44), channel_id=1, source_target_pairs={{4,8},{8,4},{12,16},{16,12},{20,24},{24,20},{5,9},{9,5},{13,17},{1... | collective-permute-start | bytes 4616 | tf_op jit(solution)/shard_map/ppermute | solution.py:337
where the time goes:
time: 49.5 us; the launch traced here: 49.2 us
  blocking collectives  24.3 us (49%)
  starting transfers between devices  9.18 us (19%)
  Pallas kernels  8.41 us (17%)
  waiting for transfers between devices  6.55 us (13%)
  between operations  0.7 us (1%)
    all_to_all x1, blocking collectives, on_device(): got = lax.all_to_all(sent, AXES, 0, 0)  15.4 us
    all_to_all x1, blocking collectives, on_device(): got = lax.all_to_all(sent, AXES, 0, 0, tiled=True)  8.89 us
    pallas_call x6, Pallas kernels, call(): pl.pallas_call(body, out_shape=tuple(outs), in_specs=[hbm] * len(fetched)...  8.41 us
    all_to_all x1, starting transfers between devices, on_device(): got = lax.all_to_all(sent, AXES, 0, 0)  7.33 us
    all_to_all x1, waiting for transfers between devices, on_device(): got = lax.all_to_all(sent, AXES, 0, 0)  4.71 us
    ppermute x2, waiting for transfers between devices, pair_exchange(): inner_value = lax.ppermute(inner_value, axis, inner)  1.84 us
    ppermute x2, starting transfers between devices, pair_exchange(): outer_value = lax.ppermute(outer_value, axis, outer)  1.31 us
  transfers between devices with their start and end apart: 5, of which 3 were waited for; matrix products, arithmetic and copies ran while one was open for 0% of the time, Pallas kernels for 5%

commit v1 on v0

--- a/solution.py
+++ b/solution.py
@@ -11,7 +11,7 @@
 F32 = jnp.float32
 BF16 = jnp.bfloat16
 VMEM_LIMIT = 12 << 20
-PIECES = 4
+PIECES = 2
 
 
 ROWS = (((1,), (0,)), ((), ()))
@@ -55,7 +55,7 @@
     return pltpu.HBM(shape, dtype)
 
 
-def call(body, outs, arrays, flops, scratch=(), fetched=(), written=False):
+def call(body, outs, arrays, flops, scratch=(), fetched=(), written=0):
     vmem = pl.BlockSpec(memory_space=pltpu.VMEM)
     hbm = pl.BlockSpec(memory_space=pltpu.HBM)
     size = sum(a.size * a.dtype.itemsize for a in arrays)
@@ -64,7 +64,7 @@
         body,
         out_shape=tuple(outs),
         in_specs=[hbm] * len(fetched) + [vmem] * len(arrays),
-        out_specs=(hbm if written else vmem,) * len(outs),
+        out_specs=(hbm,) * written + (vmem,) * (len(outs) - written),
         scratch_shapes=scratch,
         compiler_params=pltpu.CompilerParams(vmem_limit_bytes=VMEM_LIMIT),
         cost_estimate=pl.CostEstimate(flops=flops, bytes_accessed=size, transcendentals=0),
@@ -99,36 +99,48 @@
 
 def project_kernel(
     leaf_t, node_t, values_hbm, basis_hbm, conduct_hbm,
-    sent, own, wide_high, wide_low, up_high, up_low, moves, values, conduct, basis, sems,
+    sent_hbm, own, wide_high, wide_low, up_high, up_low, moves, values, conduct, basis, sent, sems,
 ):
     levels, rank = moves.shape[0], moves.shape[1]
     piece = basis.shape[0] // PIECES
-    pairs = [(values_hbm, values), (leaf_t, moves.at[0]), (node_t, moves.at[pl.ds(1, levels - 1)])]
+    slabs = [slice(i * piece, (i + 1) * piece) for i in range(PIECES)]
+    pairs = [(leaf_t, moves.at[0]), (node_t, moves.at[pl.ds(1, levels - 1)]), (values_hbm, values)]
     pairs += [(basis_hbm.at[pl.ds(i * piece, piece)], basis.at[pl.ds(i * piece, piece)]) for i in range(PIECES)]
-    pairs += [(conduct_hbm, conduct)]
+    pairs += [(conduct_hbm, conduct), (sent, sent_hbm)]
     copies = [pltpu.make_async_copy(source, target, sems.at[i]) for i, (source, target) in enumerate(pairs)]
-    for copy in copies:
+    for copy in copies[:-1]:
         copy.start()
-    for copy in copies[:3]:
-        copy.wait()
+    copies[2].wait()
     rows = flat(values)
     coeffs = jnp.zeros(own.shape, F32)
-    up = moves[0]
-    up_high[:, 0:rank], up_low[:, 0:rank] = parts(up)
-    for i in range(max(PIECES, levels - 1)):
-        if i < PIECES:
-            copies[3 + i].wait()
-            at = slice(i * piece, (i + 1) * piece)
-            held = basis[at, :]
-            coeffs = coeffs + rows_times(rows[:, at], *parts(held))
-            wide_high[:, at], wide_low[:, at] = parts(held.T)
-        if i + 1 < levels:
-            up = product(up, moves[i + 1])
-            at = slice((i + 1) * rank, (i + 2) * rank)
-            up_high[:, at], up_low[:, at] = parts(up)
+    copies[0].wait()
+    copies[1].wait()
+    ups = [moves[0]]
+    both = [product(moves[h], moves[h + 1]) for h in range(0, levels - 1, 2)]
+    waiting = list(enumerate(slabs))
+    while len(ups) < levels:
+        h = len(ups) - 1
+        if h % 2 == 0:
+            ups.append(product(ups[h - 1], both[h // 2]) if h else both[0])
+            if waiting:
+                i, at = waiting.pop(0)
+                copies[3 + i].wait()
+                coeffs = coeffs + rows_times(rows[:, at], *parts(basis[at, :]))
+        else:
+            ups.append(product(ups[h], moves[h + 1]))
+    for i, at in waiting:
+        copies[3 + i].wait()
+        coeffs = coeffs + rows_times(rows[:, at], *parts(basis[at, :]))
+    for h in range(levels):
+        at = slice(h * rank, (h + 1) * rank)
+        up_high[:, at], up_low[:, at] = parts(ups[h])
     own[...] = coeffs
     send_chain(sent, coeffs, up_high, up_low)
-    copies[3 + PIECES].wait()
+    copies[-1].start()
+    for at in slabs:
+        wide_high[:, at], wide_low[:, at] = parts(basis[at, :].T)
+    copies[-2].wait()
+    copies[-1].wait()
 
 
 def send_chain(sent, coeffs, up_high, up_low):
@@ -154,12 +166,13 @@
     copies[0].wait()
     copies[1].wait()
     total = [fronts[0]] + [product(fronts[h + 1], back[h]) for h in range(levels)]
-    copies[2].wait()
     for h in range(levels, -1, -1):
+        if h == levels // 2:
+            copies[2].wait()
+            leaf_map(values, inverse, near, held)
         if h < levels:
             total[h] = total[h] + product(moves[h], total[h + 1])
         down_high[columns[h], :], down_low[columns[h], :] = parts(total[h])
-    leaf_map(values, inverse, near, held)
 
 
 def tree(got, own, down_high, down_low):
@@ -205,12 +218,13 @@
     head, tail = edge_column(values, cond, 0), edge_column(values, cond, extent_y - 1)
     y_inner[...] = jnp.where(odd_y, head, tail)
     y_outer[...] = jnp.where(odd_y, tail, head)
-    sums[...] = jnp.sum(right[...] * values, axis=(1, 2))[:, None] * jnp.ones((1, extent_y), F32)
+    for s in range(count_s):
+        sums[s : s + 1, :] = jnp.broadcast_to(jnp.sum(right[s] * values[s]), (1, extent_y))
 
 
 def second_kernel(
-    x_inner, x_outer, y_inner, y_outer, z, conduct, wide_high, wide_low, sums, up_high, up_low, inverse,
-    applied, near, sent, own, held,
+    x_inner, x_outer, y_inner, y_outer, z, conduct, wide_high, wide_low, up_high, up_low, inverse,
+    applied, near, sent, own, curvature, held,
 ):
     count_s, extent_x, extent_y = z.shape
     odd_x, odd_y = odd("gx"), odd("gy")
@@ -231,61 +245,54 @@
 
     cond = conduct[...]
     weights = [0.5 * (cond + other) for other in beside(cond, count_s)]
-    lanes = lax.broadcasted_iota(jnp.int32, (1, extent_y), 1)
-    packed = []
     for s in range(count_s):
         values = z[s]
         total = jnp.zeros(shape, F32)
         for weight, other in zip(weights, beside(values, s)):
             total = total + weight * (values - other)
         applied[s] = total
-        curvature = jnp.sum(values * total)
-        packed.append(jnp.where(lanes == 0, sums[s : s + 1, :], jnp.where(lanes == 1, curvature, 0.0)))
+        curvature[s : s + 1, :] = jnp.broadcast_to(jnp.sum(values * total), (1, extent_y))
+    leaf_map(applied, inverse, near, held)
     coeffs = rows_times(flat(applied), wide_high[...], wide_low[...], LANES)
     own[...] = coeffs
     send_chain(sent, coeffs, up_high, up_low)
-    scalars = jnp.concatenate(packed, axis=0)
-    sent[:, count_s:, :] = jnp.broadcast_to(scalars[None], (sent.shape[0],) + scalars.shape)
-    leaf_map(applied, inverse, near, held)
 
 
 def third_kernel(
-    got, own, down_high, down_low, wide_high, wide_low, near, z, right, applied,
-    sent, totals, solution, residual, partial_d, far,
-):
-    count_s = own.shape[0]
+    got, own, down_high, down_low, wide_high, wide_low, near, applied, sums, curvature, sent, mapped
+):
     spread = tree(got, own, down_high, down_low)
-    scalars = jnp.sum(got[:, count_s:, :], axis=0)
-    totals[...] = scalars
-    square = jnp.sum(near[...] * applied[...], axis=(1, 2)) + jnp.sum(own[...] * spread, axis=1)
     lanes = lax.broadcasted_iota(jnp.int32, (1, sent.shape[1]), 1)
     row = jnp.zeros((1, sent.shape[1]), F32)
-    for s in range(count_s):
-        row = jnp.where(lanes == s, square[s], row)
+    count_s = own.shape[0]
+    for s in range(count_s):
+        square = jnp.sum(near[s] * applied[s]) + jnp.sum(own[s : s + 1, :] * spread[s : s + 1, :])
+        row = jnp.where(lanes == s, square, row)
+        row = jnp.where(lanes == count_s + s, curvature[s : s + 1, :], row)
+        row = jnp.where(lanes == 2 * count_s + s, sums[s : s + 1, :], row)
     sent[...] = jnp.broadcast_to(row, sent.shape)
-    expand_into(far, spread, wide_high, wide_low, near)
-    for s in range(count_s):
-        step = scalars[s : s + 1, 0:1] / scalars[s : s + 1, 1:2]
-        solution[s] = step * z[s]
-        residual[s] = right[s] - step * applied[s]
-        partial_d[s] = z[s] - step * far[s]
-
-
-def last_kernel(got, totals, z, partial_d, solution, residual, solution_hbm, residual_hbm, direction_hbm, direction, sems):
+    expand_into(mapped, spread, wide_high, wide_low, near)
+
+
+def last_kernel(
+    got, z, right, applied, mapped, solution_hbm, residual_hbm, direction_hbm, solution, residual, direction, sems
+):
+    count_s = z.shape[0]
     copies = [
         pltpu.make_async_copy(solution, solution_hbm, sems.at[0]),
         pltpu.make_async_copy(residual, residual_hbm, sems.at[1]),
         pltpu.make_async_copy(direction, direction_hbm, sems.at[2]),
     ]
-    copies[0].start()
-    copies[1].start()
-    square = jnp.sum(got[...], axis=0, keepdims=True)
-    for s in range(z.shape[0]):
-        curvature = totals[s : s + 1, 1:2]
-        step = totals[s : s + 1, 0:1] / curvature
-        ratio = step * square[0:1, s : s + 1] / curvature - 1.0
-        direction[s] = partial_d[s] + ratio * z[s]
-    copies[2].start()
+    totals = jnp.sum(got[...], axis=0, keepdims=True)
+    for s in range(count_s):
+        curvature = totals[0:1, count_s + s : count_s + s + 1]
+        step = totals[0:1, 2 * count_s + s : 2 * count_s + s + 1] / curvature
+        ratio = step * totals[0:1, s : s + 1] / curvature - 1.0
+        solution[s] = step * z[s]
+        residual[s] = right[s] - step * applied[s]
+        direction[s] = z[s] - step * mapped[s] + ratio * z[s]
+    for copy in copies:
+        copy.start()
     for copy in copies:
         copy.wait()
 
@@ -374,8 +381,13 @@
         ),
         (),
         10**6,
-        (pltpu.VMEM((cells, rank), F32), pltpu.SemaphoreType.DMA((4 + PIECES,))),
+        (
+            pltpu.VMEM((cells, rank), F32),
+            pltpu.VMEM((count, count_s, rank), F32),
+            pltpu.SemaphoreType.DMA((5 + PIECES,)),
+        ),
         (leaf_t, node_t, right_side, basis, conductivity),
+        written=1,
     )
     got = lax.all_to_all(sent, AXES, 0, 0)
     held = pltpu.VMEM((LBX, count_s * extent_x // LBX, extent_y), F32)
@@ -396,29 +408,34 @@
     )
     x_inner, x_outer = pair_exchange(x_inner, x_outer, "gx")
     y_inner, y_outer = pair_exchange(y_inner, y_outer, "gy")
-    applied, near, sent, own = call(
+    applied, near, sent, own, curvature = call(
         second_kernel,
-        (in_vmem(*field), in_vmem(*field), in_vmem(count, 2 * count_s, rank), in_vmem(count_s, rank)),
-        (x_inner, x_outer, y_inner, y_outer, first_z, conductivity, wide_high, wide_low, sums, up_high, up_low, inverse),
+        (
+            in_vmem(*field),
+            in_vmem(*field),
+            in_vmem(count, count_s, rank),
+            in_vmem(count_s, rank),
+            in_vmem(count_s, extent_y),
+        ),
+        (x_inner, x_outer, y_inner, y_outer, first_z, conductivity, wide_high, wide_low, up_high, up_low, inverse),
         10**6,
         (held,),
     )
     got = lax.all_to_all(sent, AXES, 0, 0)
-    sent, totals, step_z, residual, partial_d = call(
+    sent, mapped = call(
         third_kernel,
-        (in_vmem(count, rank), in_vmem(count_s, rank), in_vmem(*field), in_vmem(*field), in_vmem(*field)),
-        (got, own, down_high, down_low, wide_high, wide_low, near, first_z, right_side, applied),
+        (in_vmem(count, extent_y), in_vmem(*field)),
+        (got, own, down_high, down_low, wide_high, wide_low, near, applied, sums, curvature),
         10**6,
-        (pltpu.VMEM(field, F32),),
     )
     got = lax.all_to_all(sent, AXES, 0, 0, tiled=True)
     return call(
         last_kernel,
         (in_hbm(*field),) * 3,
-        (got, totals, first_z, partial_d, step_z, residual),
+        (got, first_z, right_side, applied, mapped),
         10**6,
-        (pltpu.VMEM(field, F32), pltpu.SemaphoreType.DMA((3,))),
-        written=True,
+        (pltpu.VMEM(field, F32),) * 3 + (pltpu.SemaphoreType.DMA((3,)),),
+        written=3,
     )
 
 

time: 49.5 us -> 48.9 us (0.988)
  no operation moved by 1% of the time
where the time goes in v1:
time: 48.9 us; the launch traced here: 48.6 us
  blocking collectives  24.1 us (49%)
  starting transfers between devices  9.17 us (19%)
  Pallas kernels  8.08 us (17%)
  waiting for transfers between devices  6.54 us (13%)
  between operations  0.71 us (1%)
    all_to_all x1, blocking collectives, on_device(): got = lax.all_to_all(sent, AXES, 0, 0)  15.2 us
    all_to_all x1, blocking collectives, on_device(): got = lax.all_to_all(sent, AXES, 0, 0, tiled=True)  8.89 us
    pallas_call x6, Pallas kernels, call(): pl.pallas_call(body, out_shape=tuple(outs), in_specs=[hbm] * len(fetched)...  8.08 us
    all_to_all x1, starting transfers between devices, on_device(): got = lax.all_to_all(sent, AXES, 0, 0)  7.33 us
    all_to_all x1, waiting for transfers between devices, on_device(): got = lax.all_to_all(sent, AXES, 0, 0)  4.7 us
    ppermute x2, waiting for transfers between devices, pair_exchange(): inner_value = lax.ppermute(inner_value, axis, inner)  1.84 us
    ppermute x2, starting transfers between devices, pair_exchange(): outer_value = lax.ppermute(outer_value, axis, outer)  1.31 us
  transfers between devices with their start and end apart: 5, of which 3 were waited for; matrix products, arithmetic and copies ran while one was open for 0% of the time, Pallas kernels for 5%

profile of v1, /device:TPU:0, one launch (start us, length us, event | category | flops | bytes accessed | tf_op | source)
XLA Modules:
  0.0 48.6 jit_solution(2815133383320980672)
XLA Ops:
  0.6 2.6 %shard_map.103 = (f32[32,2,128]{2,1,0:T(2,128)}, f32[2,128]{1,0:T(2,128)S(1)}, bf16[128,2048]{1,0:T(8,128)(2,1)S(1)}, bf16[128,2048]{1,0:T(8,128)(2,1)S(1)}, bf1...) custom-call(f32[128,128]{1,0:T(8,128)} %bitcast.14, ...), custom_call_target="tpu_custom_call" | custom-call | flops 1000000 | tf_op jit(solution)/shard_map/pallas_call | solution.py:63
  3.3 7.3 %all-to-all-start = ((f32[32,2,128]{2,1,0:T(2,128)}), f32[32,2,128]{2,1,0:T(2,128)S(1)}, u32[]{:S(2)}, u32[]{:S(2)}) async-start(f32[32,2,128]{2,1,0:T(2,128)} %get-tuple-element.29), calls=%async_computation | async-start | bytes 65536 | tf_op jit(solution)/shard_map/all_to_all | solution.py:392
  10.6 2.6 %shard_map.104 = (f32[2,16,128]{2,1,0:T(8,128)S(1)}, bf16[768,128]{1,0:T(8,128)(2,1)S(1)}, bf16[768,128]{1,0:T(8,128)(2,1)S(1)}, f32[4,4,128,128]{3,2,1,0:T(8,128)S(1)}) custom-call(f32[128,128]{1,0:T(8,128)} %bitcast.15, f32[5,128,128]{2,1,0:T(8,128)} %bitcast.12, f32[4,4,128,128]{3,2,1,0:T(8,128)} %inverse_hbm.1, ...), custom_call_target="tpu_custom_call" | custom-call | flops 10000000 | bytes 671744 | tf_op jit(solution)/shard_map/pallas_call | solution.py:63
  13.2 4.7 %all-to-all-done.got = f32[32,2,128]{2,1,0:T(2,128)S(1)} async-done(((f32[32,2,128]{2,1,0:T(2,128)}), f32[32,2,128]{2,1,0:T(2,128)S(1)}, u32[]{:S(2)}, u32[]{:S(2)}) %all-to-all-start) | async-done | bytes 32800 | tf_op jit(solution)/shard_map/all_to_all | solution.py:392
  17.9 0.6 %shard_map.105 = (f32[2,16,128]{2,1,0:T(8,128)S(1)}, f32[3,128]{1,0:T(4,128)S(1)}, f32[3,128]{1,0:T(4,128)S(1)}, f32[16,128]{1,0:T(8,128)S(1)}, f32[16,128]{1,0:T(8,128)S(1)}, /*index=5*/f32[2,128]{1,0:T(2,128)S(1)}) custom-call(f32[32,2,128]{2,1,0:T(2,128)S(1)} %all-to-all-done.got, f32[2,128]{1,0:T(2,128)S(1)} %get-tuple-element.30.own, ...), custom_call_target="tpu_custom_call" | custom-call | flops 1000000 | bytes 1516544 | tf_op jit(solution)/shard_map/pallas_call | solution.py:63
  18.5 0.5 collective-permute-start.2
  19.0 0.6 %collective-permute-start.3 = (f32[16,128]{1,0:T(8,128)S(1)}, f32[16,128]{1,0:T(8,128)S(1)}, u32[]{:S(2)}, u32[]{:S(2)}) collective-permute-start(f32[16,128]{1,0:T(8,128)S(1)} %get-tuple-element.44), channel_id=1, source_target_pairs={{1,2},{2,1},{5,6},{6,5},{9,10},{10,9},{13,14},{14,13},{17,18},{18,... | collective-permute-start | bytes 24584 | tf_op jit(solution)/shard_map/ppermute | solution.py:344
  19.6 0.1 collective-permute-start
  19.7 0.7 %collective-permute-start.1 = (f32[3,128]{1,0:T(4,128)S(1)}, f32[3,128]{1,0:T(4,128)S(1)}, u32[]{:S(2)}, u32[]{:S(2)}) collective-permute-start(f32[3,128]{1,0:T(4,128)S(1)} %get-tuple-element.42), channel_id=1, source_target_pairs={{4,8},{8,4},{12,16},{16,12},{20,24},{24,20},{5,9},{9,5},{13,17},{1... | collective-permute-start | bytes 4616 | tf_op jit(solution)/shard_map/ppermute | solution.py:344
  20.4 0.5 collective-permute-done.x_inner
  20.8 0.0 collective-permute-done.1.x_outer
  20.9 1.4 %collective-permute-done.2.y_inner = f32[16,128]{1,0:T(8,128)S(1)} collective-permute-done((f32[16,128]{1,0:T(8,128)S(1)}, f32[16,128]{1,0:T(8,128)S(1)}, u32[]{:S(2)}, u32[]{:S(2)}) %collective-permute-start.2) | collective-permute-done | bytes 8224 | tf_op jit(solution)/shard_map/ppermute | solution.py:343
  22.2 0.0 collective-permute-done.3.y_outer
  22.2 1.0 %shard_map.106 = (f32[2,16,128]{2,1,0:T(8,128)S(1)}, f32[2,16,128]{2,1,0:T(8,128)S(1)}, f32[32,2,128]{2,1,0:T(2,128)S(1)}, f32[2,128]{1,0:T(2,128)S(1)}, f32[2,128]{1,0:T(2,128)S(1)}) custom-call(f32[3,128]{1,0:T(4,128)S(1)} %collective-permute-done.x_inner, f32[3,128]{1,0:T(4,128)S(1)} %collective-permute-done.1.x_outer, ...), custom_call_target="tpu_custom_call" | custom-call | flops 1000000 | bytes 2468864 | tf_op jit(solution)/shard_map/pallas_call | solution.py:63
  23.2 15.2 %all_to_all.21.got = f32[32,2,128]{2,1,0:T(2,128)S(1)} all-to-all(f32[32,2,128]{2,1,0:T(2,128)S(1)} %get-tuple-element.47), channel_id=1, replica_groups=mesh['gx'=8,'gy'=4] {'gx','gy'}, dimensions={0} | all-to-all | bytes 65536 | tf_op jit(solution)/shard_map/all_to_all | solution.py:424
  38.4 0.5 shard_map.107
  38.9 8.9 %all_to_all.22 = f32[32,1,128]{2,1,0:T(1,128)S(1)} all-to-all(f32[32,1,128]{2,1,0:T(1,128)S(1)} %bitcast.10), channel_id=1, replica_groups=mesh['gx'=8,'gy'=4] {'gx','gy'}, dimensions={0} | all-to-all | bytes 32768 | tf_op jit(solution)/shard_map/all_to_all | solution.py:431
  47.8 0.8 %shard_map.108 = (f32[2,16,128]{2,1,0:T(8,128)}, f32[2,16,128]{2,1,0:T(8,128)}, f32[2,16,128]{2,1,0:T(8,128)}) custom-call(f32[32,128]{1,0:T(8,128)S(1)} %bitcast.9, f32[2,16,128]{2,1,0:T(8,128)S(1)} %get-tuple-element.45.z, f32[2,16,128]{2,1,0:T(8,128)S(1)} %get-tuple-element.31.values.right, f32[2,16,128]{2,1,0:T(8,128)S(1)} %get-tuple-element.50.applied, ...), custom_call_target="tpu_custom_call" | custom-call | flops 1000000 | bytes 81920 | tf_op jit(solution)/shard_map/pallas_call | solution.py:63
Async XLA Ops:
  3.3 14.6 %all-to-all-start = ((f32[32,2,128]{2,1,0:T(2,128)}), f32[32,2,128]{2,1,0:T(2,128)S(1)}, u32[]{:S(2)}, u32[]{:S(2)}) async-start(f32[32,2,128]{2,1,0:T(2,128)} %get-tuple-element.29), calls=%async_computation | async-start | bytes 65536 | tf_op jit(solution)/shard_map/all_to_all | solution.py:392
  18.5 3.7 %collective-permute-start.2 = (f32[16,128]{1,0:T(8,128)S(1)}, f32[16,128]{1,0:T(8,128)S(1)}, u32[]{:S(2)}, u32[]{:S(2)}) collective-permute-start(f32[16,128]{1,0:T(8,128)S(1)} %get-tuple-element.43), channel_id=1, source_target_pairs={{0,1},{1,0},{2,3},{3,2},{4,5},{5,4},{6,7},{7,6},{8,9},{9,8},{10,11... | collective-permute-start | bytes 24584 | tf_op jit(solution)/shard_map/ppermute | solution.py:343
  19.0 3.3 %collective-permute-start.3 = (f32[16,128]{1,0:T(8,128)S(1)}, f32[16,128]{1,0:T(8,128)S(1)}, u32[]{:S(2)}, u32[]{:S(2)}) collective-permute-start(f32[16,128]{1,0:T(8,128)S(1)} %get-tuple-element.44), channel_id=1, source_target_pairs={{1,2},{2,1},{5,6},{6,5},{9,10},{10,9},{13,14},{14,13},{17,18},{18,... | collective-permute-start | bytes 24584 | tf_op jit(solution)/shard_map/ppermute | solution.py:344
  19.6 1.2 %collective-permute-start = (f32[3,128]{1,0:T(4,128)S(1)}, f32[3,128]{1,0:T(4,128)S(1)}, u32[]{:S(2)}, u32[]{:S(2)}) collective-permute-start(f32[3,128]{1,0:T(4,128)S(1)} %get-tuple-element.41), channel_id=1, source_target_pairs={{0,4},{4,0},{8,12},{12,8},{16,20},{20,16},{24,28},{28,24},{1,5},{5... | collective-permute-start | bytes 4616 | tf_op jit(solution)/shard_map/ppermute | solution.py:343
  19.7 1.2 %collective-permute-start.1 = (f32[3,128]{1,0:T(4,128)S(1)}, f32[3,128]{1,0:T(4,128)S(1)}, u32[]{:S(2)}, u32[]{:S(2)}) collective-permute-start(f32[3,128]{1,0:T(4,128)S(1)} %get-tuple-element.42), channel_id=1, source_target_pairs={{4,8},{8,4},{12,16},{16,12},{20,24},{24,20},{5,9},{9,5},{13,17},{1... | collective-permute-start | bytes 4616 | tf_op jit(solution)/shard_map/ppermute | solution.py:344

commit v2 on v1

--- a/solution.py
+++ b/solution.py
@@ -73,6 +73,11 @@
 
 def place():
     return lax.axis_index("gx") * lax.axis_size("gy") + lax.axis_index("gy")
+
+
+def at_end(axis):
+    at = lax.axis_index(axis)
+    return jnp.logical_or(at == 0, at == lax.axis_size(axis) - 1)
 
 
 def odd(axis):
@@ -228,10 +233,12 @@
 ):
     count_s, extent_x, extent_y = z.shape
     odd_x, odd_y = odd("gx"), odd("gy")
-    above = jnp.where(odd_x, x_inner[...], x_outer[...])
-    below = jnp.where(odd_x, x_outer[...], x_inner[...])
-    before = jnp.where(odd_y, y_inner[...], y_outer[...])
-    after = jnp.where(odd_y, y_outer[...], y_inner[...])
+    x_far = jnp.where(at_end("gx"), 0.0, x_outer[...])
+    y_far = jnp.where(at_end("gy"), 0.0, y_outer[...])
+    above = jnp.where(odd_x, x_inner[...], x_far)
+    below = jnp.where(odd_x, x_far, x_inner[...])
+    before = jnp.where(odd_y, y_inner[...], y_far)
+    after = jnp.where(odd_y, y_far, y_inner[...])
     shape = (extent_x, extent_y)
     row = lax.broadcasted_iota(jnp.int32, shape, 0)
     lane = lax.broadcasted_iota(jnp.int32, shape, 1)
@@ -334,15 +341,30 @@
                 out[s, p * LBX + a : p * LBX + a + 1, :] = held[a, s * blocks_x + p : s * blocks_x + p + 1, :]
 
 
-def pair_exchange(inner_value, outer_value, axis):
-    count = lax.axis_size(axis)
-    inner = [(i, i ^ 1) for i in range(count)]
-    outer = []
-    for i in range(1, count - 1, 2):
-        outer += [(i, i + 1), (i + 1, i)]
-    inner_value = lax.ppermute(inner_value, axis, inner)
-    outer_value = lax.ppermute(outer_value, axis, outer)
-    return inner_value, outer_value
+def swap(value, pairs):
+    return lax.ppermute(value, AXES, pairs + [(j, i) for i, j in pairs])
+
+
+def matchings():
+    wide, deep = lax.axis_size("gx"), lax.axis_size("gy")
+
+    def along(first, second):
+        return [
+            ((i, j), (i + di, j + dj))
+            for i in range(first[0], first[1], first[2])
+            for j in range(second[0], second[1], second[2])
+            for di, dj in [(first[3], second[3])]
+        ]
+
+    everywhere_x, everywhere_y = (0, wide, 1, 0), (0, deep, 1, 0)
+    ends_x, ends_y = (0, wide, max(wide - 1, 1), 0), (0, deep, max(deep - 1, 1), 0)
+    sets = {
+        "gx_inner": along((0, wide - 1, 2, 1), everywhere_y),
+        "gx_outer": along((1, wide - 1, 2, 1), everywhere_y) + along(ends_x, (0, deep - 1, 2, 1)),
+        "gy_inner": along(everywhere_x, (0, deep - 1, 2, 1)),
+        "gy_outer": along(everywhere_x, (1, deep - 1, 2, 1)) + along((0, wide - 1, 2, 1), ends_y),
+    }
+    return {name: [(i * deep + j, k * deep + l) for (i, j), (k, l) in pairs] for name, pairs in sets.items()}
 
 
 def on_device(
@@ -406,8 +428,9 @@
         (got, own, down_high, down_low, wide_high, wide_low, near, right_side, conductivity),
         10**6,
     )
-    x_inner, x_outer = pair_exchange(x_inner, x_outer, "gx")
-    y_inner, y_outer = pair_exchange(y_inner, y_outer, "gy")
+    pairs = matchings()
+    x_inner, x_outer = swap(x_inner, pairs["gx_inner"]), swap(x_outer, pairs["gx_outer"])
+    y_inner, y_outer = swap(y_inner, pairs["gy_inner"]), swap(y_outer, pairs["gy_outer"])
     applied, near, sent, own, curvature = call(
         second_kernel,
         (

time: 48.9 us -> 45 us (0.920)
  blocking collectives: 24.1 us -> 19.4 us
  waiting for transfers between devices: 6.54 us -> 7.16 us
    all_to_all x1, blocking collectives: 15.2 us -> 10.5 us  [on_device(): got = lax.all_to_all(sent, AXES, 0, 0)]
    ppermute x4, waiting for transfers between devices: 1.85 us -> 2.47 us  [swap(): return lax.ppermute(value, AXES, pairs + [(j, i) for i, j in pairs])]
  transfers between devices with their start and end apart: 5 -> 5, of which waited for: 3 -> 2; matrix products, arithmetic and copies ran while one was open for 0% -> 0% of each run, Pallas kernels for 5% -> 6%
where the time goes in v2:
time: 45 us; the launch traced here: 44.8 us
  blocking collectives  19.4 us (43%)
  starting transfers between devices  9.43 us (21%)
  Pallas kernels  8.08 us (18%)
  waiting for transfers between devices  7.16 us (16%)
  between operations  0.68 us (2%)
    all_to_all x1, blocking collectives, on_device(): got = lax.all_to_all(sent, AXES, 0, 0)  10.5 us
    all_to_all x1, blocking collectives, on_device(): got = lax.all_to_all(sent, AXES, 0, 0, tiled=True)  8.89 us
    pallas_call x6, Pallas kernels, call(): pl.pallas_call(body, out_shape=tuple(outs), in_specs=[hbm] * len(fetched)...  8.08 us
    all_to_all x1, starting transfers between devices, on_device(): got = lax.all_to_all(sent, AXES, 0, 0)  7.33 us
    all_to_all x1, waiting for transfers between devices, on_device(): got = lax.all_to_all(sent, AXES, 0, 0)  4.7 us
    ppermute x4, waiting for transfers between devices, swap(): return lax.ppermute(value, AXES, pairs + [(j, i) for i, j in pairs])  2.47 us
    ppermute x4, starting transfers between devices, swap(): return lax.ppermute(value, AXES, pairs + [(j, i) for i, j in pairs])  2.1 us
  transfers between devices with their start and end apart: 5, of which 2 were waited for; matrix products, arithmetic and copies ran while one was open for 0% of the time, Pallas kernels for 6%

profile of v2, /device:TPU:0, one launch (start us, length us, event | category | flops | bytes accessed | tf_op | source)
XLA Modules:
  0.0 44.8 jit_solution(3351612842184920504)
XLA Ops:
  0.6 2.6 %shard_map.103 = (f32[32,2,128]{2,1,0:T(2,128)}, f32[2,128]{1,0:T(2,128)S(1)}, bf16[128,2048]{1,0:T(8,128)(2,1)S(1)}, bf16[128,2048]{1,0:T(8,128)(2,1)S(1)}, bf1...) custom-call(f32[128,128]{1,0:T(8,128)} %bitcast.14, ...), custom_call_target="tpu_custom_call" | custom-call | flops 1000000 | tf_op jit(solution)/shard_map/pallas_call | solution.py:63
  3.3 7.3 %all-to-all-start = ((f32[32,2,128]{2,1,0:T(2,128)}), f32[32,2,128]{2,1,0:T(2,128)S(1)}, u32[]{:S(2)}, u32[]{:S(2)}) async-start(f32[32,2,128]{2,1,0:T(2,128)} %get-tuple-element.29), calls=%async_computation | async-start | bytes 65536 | tf_op jit(solution)/shard_map/all_to_all | solution.py:414
  10.6 2.6 %shard_map.104 = (f32[2,16,128]{2,1,0:T(8,128)S(1)}, bf16[768,128]{1,0:T(8,128)(2,1)S(1)}, bf16[768,128]{1,0:T(8,128)(2,1)S(1)}, f32[4,4,128,128]{3,2,1,0:T(8,128)S(1)}) custom-call(f32[128,128]{1,0:T(8,128)} %bitcast.15, f32[5,128,128]{2,1,0:T(8,128)} %bitcast.12, f32[4,4,128,128]{3,2,1,0:T(8,128)} %inverse_hbm.1, ...), custom_call_target="tpu_custom_call" | custom-call | flops 10000000 | bytes 671744 | tf_op jit(solution)/shard_map/pallas_call | solution.py:63
  13.2 4.7 %all-to-all-done.got = f32[32,2,128]{2,1,0:T(2,128)S(1)} async-done(((f32[32,2,128]{2,1,0:T(2,128)}), f32[32,2,128]{2,1,0:T(2,128)S(1)}, u32[]{:S(2)}, u32[]{:S(2)}) %all-to-all-start) | async-done | bytes 32800 | tf_op jit(solution)/shard_map/all_to_all | solution.py:414
  17.9 0.6 %shard_map.105 = (f32[2,16,128]{2,1,0:T(8,128)S(1)}, f32[3,128]{1,0:T(4,128)S(1)}, f32[3,128]{1,0:T(4,128)S(1)}, f32[16,128]{1,0:T(8,128)S(1)}, f32[16,128]{1,0:T(8,128)S(1)}, /*index=5*/f32[2,128]{1,0:T(2,128)S(1)}) custom-call(f32[32,2,128]{2,1,0:T(2,128)S(1)} %all-to-all-done.got, f32[2,128]{1,0:T(2,128)S(1)} %get-tuple-element.30.own, ...), custom_call_target="tpu_custom_call" | custom-call | flops 1000000 | bytes 1516544 | tf_op jit(solution)/shard_map/pallas_call | solution.py:63
  18.5 0.5 %collective-permute-start.2 = (f32[16,128]{1,0:T(8,128)S(1)}, f32[16,128]{1,0:T(8,128)S(1)}, u32[]{:S(2)}, u32[]{:S(2)}) collective-permute-start(f32[16,128]{1,0:T(8,128)S(1)} %get-tuple-element.43), channel_id=1, source_target_pairs={{0,1},{2,3},{4,5},{6,7},{8,9},{10,11},{12,13},{14,15},{16,17},{18,... | collective-permute-start | bytes 24584 | tf_op jit(solution)/shard_map/ppermute | solution.py:345
  19.0 0.0 collective-permute-start.3
  19.0 0.5 %collective-permute-start = (f32[3,128]{1,0:T(4,128)S(1)}, f32[3,128]{1,0:T(4,128)S(1)}, u32[]{:S(2)}, u32[]{:S(2)}) collective-permute-start(f32[3,128]{1,0:T(4,128)S(1)} %get-tuple-element.41), channel_id=1, source_target_pairs={{0,4},{1,5},{2,6},{3,7},{8,12},{9,13},{10,14},{11,15},{16,20},{17,... | collective-permute-start | bytes 4616 | tf_op jit(solution)/shard_map/ppermute | solution.py:345
  19.5 1.1 %collective-permute-start.1 = (f32[3,128]{1,0:T(4,128)S(1)}, f32[3,128]{1,0:T(4,128)S(1)}, u32[]{:S(2)}, u32[]{:S(2)}) collective-permute-start(f32[3,128]{1,0:T(4,128)S(1)} %get-tuple-element.42), channel_id=1, source_target_pairs={{4,8},{5,9},{6,10},{7,11},{12,16},{13,17},{14,18},{15,19},{20,24},... | collective-permute-start | bytes 4616 | tf_op jit(solution)/shard_map/ppermute | solution.py:345
  20.6 0.0 collective-permute-done.x_inner
  20.6 2.5 %collective-permute-done.1.x_outer = f32[3,128]{1,0:T(4,128)S(1)} collective-permute-done((f32[3,128]{1,0:T(4,128)S(1)}, f32[3,128]{1,0:T(4,128)S(1)}, u32[]{:S(2)}, u32[]{:S(2)}) %collective-permute-start.1) | collective-permute-done | bytes 1568 | tf_op jit(solution)/shard_map/ppermute | solution.py:345
  23.1 0.0 collective-permute-done.2.y_inner
  23.1 0.0 collective-permute-done.3.y_outer
  23.1 1.0 %shard_map.106 = (f32[2,16,128]{2,1,0:T(8,128)S(1)}, f32[2,16,128]{2,1,0:T(8,128)S(1)}, f32[32,2,128]{2,1,0:T(2,128)S(1)}, f32[2,128]{1,0:T(2,128)S(1)}, f32[2,128]{1,0:T(2,128)S(1)}) custom-call(f32[3,128]{1,0:T(4,128)S(1)} %collective-permute-done.x_inner, f32[3,128]{1,0:T(4,128)S(1)} %collective-permute-done.1.x_outer, ...), custom_call_target="tpu_custom_call" | custom-call | flops 1000000 | bytes 2468864 | tf_op jit(solution)/shard_map/pallas_call | solution.py:63
  24.1 10.5 %all_to_all.21.got = f32[32,2,128]{2,1,0:T(2,128)S(1)} all-to-all(f32[32,2,128]{2,1,0:T(2,128)S(1)} %get-tuple-element.47), channel_id=1, replica_groups=mesh['gx'=8,'gy'=4] {'gx','gy'}, dimensions={0} | all-to-all | bytes 65536 | tf_op jit(solution)/shard_map/all_to_all | solution.py:447
  34.6 0.5 %shard_map.107 = (f32[32,128]{1,0:T(8,128)S(1)}, f32[2,16,128]{2,1,0:T(8,128)S(1)}) custom-call(f32[32,2,128]{2,1,0:T(2,128)S(1)} %all_to_all.21.got, f32[2,128]{1,0:T(2,128)S(1)} %get-tuple-element.48.own, bf16[768,128]{1,0:T(8,128)(2,1)S(1)} %get-tuple-element.35.down_high, bf16[768,128]{1,0:T(8,128)(2,1)S(1)} %get-tuple-element.36.down_low, ...), custom_call_target="tpu_custom_call" | custom-call | flops 1000000 | bytes 1510400 | tf_op jit(solution)/shard_map/pallas_call | solution.py:63
  35.1 8.9 %all_to_all.22 = f32[32,1,128]{2,1,0:T(1,128)S(1)} all-to-all(f32[32,1,128]{2,1,0:T(1,128)S(1)} %bitcast.10), channel_id=1, replica_groups=mesh['gx'=8,'gy'=4] {'gx','gy'}, dimensions={0} | all-to-all | bytes 32768 | tf_op jit(solution)/shard_map/all_to_all | solution.py:454
  43.9 0.8 %shard_map.108 = (f32[2,16,128]{2,1,0:T(8,128)}, f32[2,16,128]{2,1,0:T(8,128)}, f32[2,16,128]{2,1,0:T(8,128)}) custom-call(f32[32,128]{1,0:T(8,128)S(1)} %bitcast.9, f32[2,16,128]{2,1,0:T(8,128)S(1)} %get-tuple-element.45.z, f32[2,16,128]{2,1,0:T(8,128)S(1)} %get-tuple-element.31.values.right, f32[2,16,128]{2,1,0:T(8,128)S(1)} %get-tuple-element.50.applied, ...), custom_call_target="tpu_custom_call" | custom-call | flops 1000000 | bytes 81920 | tf_op jit(solution)/shard_map/pallas_call | solution.py:63
Async XLA Ops:
  3.3 14.6 %all-to-all-start = ((f32[32,2,128]{2,1,0:T(2,128)}), f32[32,2,128]{2,1,0:T(2,128)S(1)}, u32[]{:S(2)}, u32[]{:S(2)}) async-start(f32[32,2,128]{2,1,0:T(2,128)} %get-tuple-element.29), calls=%async_computation | async-start | bytes 65536 | tf_op jit(solution)/shard_map/all_to_all | solution.py:414
  18.5 4.6 %collective-permute-start.2 = (f32[16,128]{1,0:T(8,128)S(1)}, f32[16,128]{1,0:T(8,128)S(1)}, u32[]{:S(2)}, u32[]{:S(2)}) collective-permute-start(f32[16,128]{1,0:T(8,128)S(1)} %get-tuple-element.43), channel_id=1, source_target_pairs={{0,1},{2,3},{4,5},{6,7},{8,9},{10,11},{12,13},{14,15},{16,17},{18,... | collective-permute-start | bytes 24584 | tf_op jit(solution)/shard_map/ppermute | solution.py:345
  19.0 4.1 %collective-permute-start.3 = (f32[16,128]{1,0:T(8,128)S(1)}, f32[16,128]{1,0:T(8,128)S(1)}, u32[]{:S(2)}, u32[]{:S(2)}) collective-permute-start(f32[16,128]{1,0:T(8,128)S(1)} %get-tuple-element.44), channel_id=1, source_target_pairs={{1,2},{5,6},{9,10},{13,14},{17,18},{21,22},{25,26},{29,30},{0,4},{... | collective-permute-start | bytes 24584 | tf_op jit(solution)/shard_map/ppermute | solution.py:345
  19.0 1.6 %collective-permute-start = (f32[3,128]{1,0:T(4,128)S(1)}, f32[3,128]{1,0:T(4,128)S(1)}, u32[]{:S(2)}, u32[]{:S(2)}) collective-permute-start(f32[3,128]{1,0:T(4,128)S(1)} %get-tuple-element.41), channel_id=1, source_target_pairs={{0,4},{1,5},{2,6},{3,7},{8,12},{9,13},{10,14},{11,15},{16,20},{17,... | collective-permute-start | bytes 4616 | tf_op jit(solution)/shard_map/ppermute | solution.py:345
  19.5 3.6 %collective-permute-start.1 = (f32[3,128]{1,0:T(4,128)S(1)}, f32[3,128]{1,0:T(4,128)S(1)}, u32[]{:S(2)}, u32[]{:S(2)}) collective-permute-start(f32[3,128]{1,0:T(4,128)S(1)} %get-tuple-element.42), channel_id=1, source_target_pairs={{4,8},{5,9},{6,10},{7,11},{12,16},{13,17},{14,18},{15,19},{20,24},... | collective-permute-start | bytes 4616 | tf_op jit(solution)/shard_map/ppermute | solution.py:345

commit v3 on v2

--- a/solution.py
+++ b/solution.py
@@ -156,7 +156,7 @@
 
 def window_kernel(
     leaf_f, node_f, inverse_hbm, values, moves, up_high, up_low,
-    near, down_high, down_low, inverse, fronts, held, sems,
+    near, down_high, down_low, meet_high, meet_low, inverse, fronts, held, sems,
 ):
     levels, rank = moves.shape[0], moves.shape[1]
     copies = [
@@ -178,6 +178,11 @@
         if h < levels:
             total[h] = total[h] + product(moves[h], total[h + 1])
         down_high[columns[h], :], down_low[columns[h], :] = parts(total[h])
+        if h > 0:
+            second = lax.rem(place() >> (h - 1), 2) == 1
+            at = columns[h - 1]
+            plain = up_high[:, at].astype(F32) + up_low[:, at].astype(F32)
+            meet_high[:, at], meet_low[:, at] = parts(jnp.where(second, total[h].T, plain))
 
 
 def tree(got, own, down_high, down_low):
@@ -228,8 +233,8 @@
 
 
 def second_kernel(
-    x_inner, x_outer, y_inner, y_outer, z, conduct, wide_high, wide_low, up_high, up_low, inverse,
-    applied, near, sent, own, curvature, held,
+    x_inner, x_outer, y_inner, y_outer, z, conduct, wide_high, wide_low, meet_high, meet_low, down_high, down_low, inverse,
+    sums, applied, near, sent, home, held,
 ):
     count_s, extent_x, extent_y = z.shape
     odd_x, odd_y = odd("gx"), odd("gy")
@@ -252,54 +257,70 @@
 
     cond = conduct[...]
     weights = [0.5 * (cond + other) for other in beside(cond, count_s)]
+    lanes = lax.broadcasted_iota(jnp.int32, (1, extent_y), 1)
+    curvature = []
     for s in range(count_s):
         values = z[s]
         total = jnp.zeros(shape, F32)
         for weight, other in zip(weights, beside(values, s)):
             total = total + weight * (values - other)
         applied[s] = total
-        curvature[s : s + 1, :] = jnp.broadcast_to(jnp.sum(values * total), (1, extent_y))
+        curvature.append(jnp.sum(values * total))
+    coeffs = rows_times(flat(applied), wide_high[...], wide_low[...], LANES)
     leaf_map(applied, inverse, near, held)
-    coeffs = rows_times(flat(applied), wide_high[...], wide_low[...], LANES)
-    own[...] = coeffs
-    send_chain(sent, coeffs, up_high, up_low)
-
-
-def third_kernel(
-    got, own, down_high, down_low, wide_high, wide_low, near, applied, sums, curvature, sent, mapped
+    rank = coeffs.shape[1]
+    chain = rows_times(coeffs, meet_high[...], meet_low[...])
+    back = rows_times(coeffs, down_high[0:rank, :], down_low[0:rank, :])
+    home[...] = back
+    levels = chain.shape[1] // rank
+    for level in range(levels):
+        row = chain[:, level * rank : (level + 1) * rank]
+        sent[:, level] = jnp.broadcast_to(row[None], (sent.shape[0],) + row.shape)
+    packed = []
+    for s in range(count_s):
+        square = jnp.sum(near[s] * applied[s]) + jnp.sum(coeffs[s : s + 1, :] * back[s : s + 1, :])
+        row = jnp.where(lanes == 0, square, jnp.where(lanes == 1, curvature[s], 0.0))
+        packed.append(jnp.where(lanes == 2, sums[s : s + 1, :], row))
+    row = jnp.concatenate(packed, axis=0)
+    sent[:, levels] = jnp.broadcast_to(row[None], (sent.shape[0],) + row.shape)
+
+
+def last_kernel(
+    got, home, meet_high, meet_low, wide_high, wide_low, near, z, right, applied,
+    solution_hbm, residual_hbm, direction_hbm, solution, residual, direction, mapped, sems,
 ):
-    spread = tree(got, own, down_high, down_low)
-    lanes = lax.broadcasted_iota(jnp.int32, (1, sent.shape[1]), 1)
-    row = jnp.zeros((1, sent.shape[1]), F32)
-    count_s = own.shape[0]
-    for s in range(count_s):
-        square = jnp.sum(near[s] * applied[s]) + jnp.sum(own[s : s + 1, :] * spread[s : s + 1, :])
-        row = jnp.where(lanes == s, square, row)
-        row = jnp.where(lanes == count_s + s, curvature[s : s + 1, :], row)
-        row = jnp.where(lanes == 2 * count_s + s, sums[s : s + 1, :], row)
-    sent[...] = jnp.broadcast_to(row, sent.shape)
-    expand_into(mapped, spread, wide_high, wide_low, near)
-
-
-def last_kernel(
-    got, z, right, applied, mapped, solution_hbm, residual_hbm, direction_hbm, solution, residual, direction, sems
-):
-    count_s = z.shape[0]
+    me = place()
+    levels, count_s = got.shape[1] - 1, got.shape[2]
     copies = [
         pltpu.make_async_copy(solution, solution_hbm, sems.at[0]),
         pltpu.make_async_copy(residual, residual_hbm, sems.at[1]),
         pltpu.make_async_copy(direction, direction_hbm, sems.at[2]),
     ]
-    totals = jnp.sum(got[...], axis=0, keepdims=True)
-    for s in range(count_s):
-        curvature = totals[0:1, count_s + s : count_s + s + 1]
-        step = totals[0:1, 2 * count_s + s : 2 * count_s + s + 1] / curvature
-        ratio = step * totals[0:1, s : s + 1] / curvature - 1.0
-        solution[s] = step * z[s]
-        residual[s] = right[s] - step * applied[s]
-        direction[s] = z[s] - step * mapped[s] + ratio * z[s]
-    for copy in copies:
-        copy.start()
+    heard, cross = [], jnp.zeros(home.shape, F32)
+    for level in range(1, levels + 1):
+        size = 1 << (level - 1)
+        heard.append(jnp.sum(got[pl.ds(cousins(me, level), size), level - 1], axis=0))
+        rows = got[:, level - 1]
+        for _ in range(level - 1):
+            rows = rows.reshape((rows.shape[0] // 2, 2) + rows.shape[1:])
+            rows = rows[:, 0] + rows[:, 1]
+        rows = rows.reshape((rows.shape[0] // 2, 2) + rows.shape[1:])
+        cross = cross + jnp.sum(rows[:, 0] * rows[:, 1], axis=0)
+    totals = jnp.sum(got[:, levels], axis=0)
+    square = totals[:, 0:1] + 2.0 * jnp.sum(cross, axis=1, keepdims=True)
+    curvature = totals[:, 1:2]
+    steps = totals[:, 2:3] / curvature
+    ratios = steps * square / curvature - 1.0
+    for s in range(count_s):
+        solution[s] = steps[s : s + 1] * z[s]
+        residual[s] = right[s] - steps[s : s + 1] * applied[s]
+    copies[0].start()
+    copies[1].start()
+    spread = home[...] + rows_times(jnp.concatenate(heard, axis=1), meet_high[...], meet_low[...], LANES)
+    expand_into(mapped, spread, wide_high, wide_low, near)
+    for s in range(count_s):
+        direction[s] = z[s] - steps[s : s + 1] * mapped[s] + ratios[s : s + 1] * z[s]
+    copies[2].start()
     for copy in copies:
         copy.wait()
 
@@ -413,9 +434,14 @@
     )
     got = lax.all_to_all(sent, AXES, 0, 0)
     held = pltpu.VMEM((LBX, count_s * extent_x // LBX, extent_y), F32)
-    near, down_high, down_low, inverse = call(
+    near, down_high, down_low, meet_high, meet_low, inverse = call(
         window_kernel,
-        (in_vmem(*field), *pair((levels + 1) * rank, rank), in_vmem(*leaf_inverse.shape)),
+        (
+            in_vmem(*field),
+            *pair((levels + 1) * rank, rank),
+            *pair(rank, levels * rank),
+            in_vmem(*leaf_inverse.shape),
+        ),
         (right_side, moves, up_high, up_low),
         10**7,
         (pltpu.VMEM((levels + 1, rank, rank), F32), held, pltpu.SemaphoreType.DMA((3,))),
@@ -431,33 +457,28 @@
     pairs = matchings()
     x_inner, x_outer = swap(x_inner, pairs["gx_inner"]), swap(x_outer, pairs["gx_outer"])
     y_inner, y_outer = swap(y_inner, pairs["gy_inner"]), swap(y_outer, pairs["gy_outer"])
-    applied, near, sent, own, curvature = call(
+    applied, near, sent, home = call(
         second_kernel,
         (
             in_vmem(*field),
             in_vmem(*field),
-            in_vmem(count, count_s, rank),
+            in_vmem(count, levels + 1, count_s, rank),
             in_vmem(count_s, rank),
-            in_vmem(count_s, extent_y),
         ),
-        (x_inner, x_outer, y_inner, y_outer, first_z, conductivity, wide_high, wide_low, up_high, up_low, inverse),
+        (
+            x_inner, x_outer, y_inner, y_outer, first_z, conductivity,
+            wide_high, wide_low, meet_high, meet_low, down_high, down_low, inverse, sums,
+        ),
         10**6,
         (held,),
     )
     got = lax.all_to_all(sent, AXES, 0, 0)
-    sent, mapped = call(
-        third_kernel,
-        (in_vmem(count, extent_y), in_vmem(*field)),
-        (got, own, down_high, down_low, wide_high, wide_low, near, applied, sums, curvature),
-        10**6,
-    )
-    got = lax.all_to_all(sent, AXES, 0, 0, tiled=True)
     return call(
         last_kernel,
         (in_hbm(*field),) * 3,
-        (got, first_z, right_side, applied, mapped),
+        (got, home, meet_high, meet_low, wide_high, wide_low, near, first_z, right_side, applied),
         10**6,
-        (pltpu.VMEM(field, F32),) * 3 + (pltpu.SemaphoreType.DMA((3,)),),
+        (pltpu.VMEM(field, F32),) * 4 + (pltpu.SemaphoreType.DMA((3,)),),
         written=3,
     )
 

time: 45 us -> 38.2 us (0.85)
  blocking collectives: 19.4 us -> 12.5 us
    all_to_all x1 -> x0, blocking collectives: 8.89 us -> none  [on_device(): got = lax.all_to_all(sent, AXES, 0, 0, tiled=True)]
    all_to_all x1, blocking collectives: 10.5 us -> 12.5 us  [on_device(): got = lax.all_to_all(sent, AXES, 0, 0)]
    pallas_call x6 -> x5, Pallas kernels: 8.08 us -> 8.26 us  [call(): pl.pallas_call(body, out_shape=tuple(outs), in_specs=[hbm] * len(fetched)...]
  transfers between devices with their start and end apart: 5 -> 5, of which waited for: 2 -> 2; matrix products, arithmetic and copies ran while one was open for 0% -> 0% of each run, Pallas kernels for 6% -> 7%
where the time goes in v3:
time: 38.2 us; the launch traced here: 38 us
  blocking collectives  12.5 us (33%)
  starting transfers between devices  9.43 us (25%)
  Pallas kernels  8.26 us (22%)
  waiting for transfers between devices  7.1 us (19%)
  between operations  0.68 us (2%)
    all_to_all x1, blocking collectives, on_device(): got = lax.all_to_all(sent, AXES, 0, 0)  12.5 us
    pallas_call x5, Pallas kernels, call(): pl.pallas_call(body, out_shape=tuple(outs), in_specs=[hbm] * len(fetched)...  8.26 us
    all_to_all x1, starting transfers between devices, on_device(): got = lax.all_to_all(sent, AXES, 0, 0)  7.33 us
    all_to_all x1, waiting for transfers between devices, on_device(): got = lax.all_to_all(sent, AXES, 0, 0)  4.63 us
    ppermute x4, waiting for transfers between devices, swap(): return lax.ppermute(value, AXES, pairs + [(j, i) for i, j in pairs])  2.47 us
    ppermute x4, starting transfers between devices, swap(): return lax.ppermute(value, AXES, pairs + [(j, i) for i, j in pairs])  2.1 us
  transfers between devices with their start and end apart: 5, of which 2 were waited for; matrix products, arithmetic and copies ran while one was open for 0% of the time, Pallas kernels for 7%

profile of v3, /device:TPU:0, one launch (start us, length us, event | category | flops | bytes accessed | tf_op | source)
XLA Modules:
  0.0 38.0 jit_solution(4244756665238255474)
XLA Ops:
  0.6 2.6 %shard_map.103 = (f32[32,2,128]{2,1,0:T(2,128)}, f32[2,128]{1,0:T(2,128)S(1)}, bf16[128,2048]{1,0:T(8,128)(2,1)S(1)}, bf16[128,2048]{1,0:T(8,128)(2,1)S(1)}, bf1...) custom-call(f32[128,128]{1,0:T(8,128)} %bitcast.8, ...), custom_call_target="tpu_custom_call" | custom-call | flops 1000000 | tf_op jit(solution)/shard_map/pallas_call | solution.py:63
  3.3 7.3 %all-to-all-start = ((f32[32,2,128]{2,1,0:T(2,128)}), f32[32,2,128]{2,1,0:T(2,128)S(1)}, u32[]{:S(2)}, u32[]{:S(2)}) async-start(f32[32,2,128]{2,1,0:T(2,128)} %get-tuple-element.28), calls=%async_computation | async-start | bytes 65536 | tf_op jit(solution)/shard_map/all_to_all | solution.py:435
  10.6 2.7 %shard_map.104 = (f32[2,16,128]{2,1,0:T(8,128)S(1)}, bf16[768,128]{1,0:T(8,128)(2,1)S(1)}, bf16[768,128]{1,0:T(8,128)(2,1)S(1)}, bf16[128,640]{1,0:T(8,128)(2,1)...) custom-call(f32[128,128]{1,0:T(8,128)} %bitcast.9, f32[5,128,128]{2,1,0:T(8,128)} %bitcast.6, ...), custom_call_target="tpu_custom_call" | custom-call | flops 10000000 | bytes 671744 | tf_op jit(solution)/shard_map/pallas_call | solution.py:63
  13.3 4.6 %all-to-all-done.got = f32[32,2,128]{2,1,0:T(2,128)S(1)} async-done(((f32[32,2,128]{2,1,0:T(2,128)}), f32[32,2,128]{2,1,0:T(2,128)S(1)}, u32[]{:S(2)}, u32[]{:S(2)}) %all-to-all-start) | async-done | bytes 32800 | tf_op jit(solution)/shard_map/all_to_all | solution.py:435
  17.9 0.6 %shard_map.105 = (f32[2,16,128]{2,1,0:T(8,128)S(1)}, f32[3,128]{1,0:T(4,128)S(1)}, f32[3,128]{1,0:T(4,128)S(1)}, f32[16,128]{1,0:T(8,128)S(1)}, f32[16,128]{1,0:T(8,128)S(1)}, /*index=5*/f32[2,128]{1,0:T(2,128)S(1)}) custom-call(f32[32,2,128]{2,1,0:T(2,128)S(1)} %all-to-all-done.got, f32[2,128]{1,0:T(2,128)S(1)} %get-tuple-element.29.own, ...), custom_call_target="tpu_custom_call" | custom-call | flops 1000000 | bytes 1516544 | tf_op jit(solution)/shard_map/pallas_call | solution.py:63
  18.5 0.5 %collective-permute-start.2 = (f32[16,128]{1,0:T(8,128)S(1)}, f32[16,128]{1,0:T(8,128)S(1)}, u32[]{:S(2)}, u32[]{:S(2)}) collective-permute-start(f32[16,128]{1,0:T(8,128)S(1)} %get-tuple-element.42), channel_id=1, source_target_pairs={{0,1},{2,3},{4,5},{6,7},{8,9},{10,11},{12,13},{14,15},{16,17},{18,... | collective-permute-start | bytes 24584 | tf_op jit(solution)/shard_map/ppermute | solution.py:366
  19.0 0.0 collective-permute-start.3
  19.0 0.5 %collective-permute-start = (f32[3,128]{1,0:T(4,128)S(1)}, f32[3,128]{1,0:T(4,128)S(1)}, u32[]{:S(2)}, u32[]{:S(2)}) collective-permute-start(f32[3,128]{1,0:T(4,128)S(1)} %get-tuple-element.40), channel_id=1, source_target_pairs={{0,4},{1,5},{2,6},{3,7},{8,12},{9,13},{10,14},{11,15},{16,20},{17,... | collective-permute-start | bytes 4616 | tf_op jit(solution)/shard_map/ppermute | solution.py:366
  19.5 1.1 %collective-permute-start.1 = (f32[3,128]{1,0:T(4,128)S(1)}, f32[3,128]{1,0:T(4,128)S(1)}, u32[]{:S(2)}, u32[]{:S(2)}) collective-permute-start(f32[3,128]{1,0:T(4,128)S(1)} %get-tuple-element.41), channel_id=1, source_target_pairs={{4,8},{5,9},{6,10},{7,11},{12,16},{13,17},{14,18},{15,19},{20,24},... | collective-permute-start | bytes 4616 | tf_op jit(solution)/shard_map/ppermute | solution.py:366
  20.6 0.0 collective-permute-done.x_inner
  20.6 2.5 %collective-permute-done.1.x_outer = f32[3,128]{1,0:T(4,128)S(1)} collective-permute-done((f32[3,128]{1,0:T(4,128)S(1)}, f32[3,128]{1,0:T(4,128)S(1)}, u32[]{:S(2)}, u32[]{:S(2)}) %collective-permute-start.1) | collective-permute-done | bytes 1568 | tf_op jit(solution)/shard_map/ppermute | solution.py:366
  23.1 0.0 collective-permute-done.2.y_inner
  23.1 0.0 collective-permute-done.3.y_outer
  23.1 1.1 %shard_map.106 = (f32[2,16,128]{2,1,0:T(8,128)S(1)}, f32[2,16,128]{2,1,0:T(8,128)S(1)}, f32[32,6,2,128]{3,2,1,0:T(2,128)S(1)}, f32[2,128]{1,0:T(2,128)S(1)}) custom-call(f32[3,128]{1,0:T(4,128)S(1)} %collective-permute-done.x_inner, f32[3,128]{1,0:T(4,128)S(1)} %collective-permute-done.1.x_outer, f32[16,128]{1,0:T(8,128)S(1)} %collective-permute-done.2.y_inner, ...), custom_call_target="tpu_custom_call" | custom-call | flops 1000000 | bytes 2863104 | tf_op jit(solution)/shard_map/pallas_call | solution.py:63
  24.1 12.5 %all_to_all.10.got = f32[32,6,2,128]{3,2,1,0:T(2,128)S(1)} all-to-all(f32[32,6,2,128]{3,2,1,0:T(2,128)S(1)} %get-tuple-element.49), channel_id=1, replica_groups=mesh['gx'=8,'gy'=4] {'gx','gy'}, dimensions={0} | all-to-all | bytes 393216 | tf_op jit(solution)/shard_map/all_to_all | solution.py:475
  36.7 1.3 %shard_map.107 = (f32[2,16,128]{2,1,0:T(8,128)}, f32[2,16,128]{2,1,0:T(8,128)}, f32[2,16,128]{2,1,0:T(8,128)}) custom-call(f32[32,6,2,128]{3,2,1,0:T(2,128)S(1)} %all_to_all.10.got, f32[2,128]{1,0:T(2,128)S(1)} %get-tuple-element.50.home, bf16[128,640]{1,0:T(8,128)(2,1)S(1)} %get-tuple-element.45.meet_high, bf16[128,640]{1,0:T(8,128)(2,1)S(1)} %get-tuple-element.46.meet_low, ...), custom_call_target="tpu_custom_call" | custom-call | flops 1000000 | bytes 1639424 | tf_op jit(solution)/shard_map/pallas_call | solution.py:63
Async XLA Ops:
  3.3 14.6 %all-to-all-start = ((f32[32,2,128]{2,1,0:T(2,128)}), f32[32,2,128]{2,1,0:T(2,128)S(1)}, u32[]{:S(2)}, u32[]{:S(2)}) async-start(f32[32,2,128]{2,1,0:T(2,128)} %get-tuple-element.28), calls=%async_computation | async-start | bytes 65536 | tf_op jit(solution)/shard_map/all_to_all | solution.py:435
  18.5 4.6 %collective-permute-start.2 = (f32[16,128]{1,0:T(8,128)S(1)}, f32[16,128]{1,0:T(8,128)S(1)}, u32[]{:S(2)}, u32[]{:S(2)}) collective-permute-start(f32[16,128]{1,0:T(8,128)S(1)} %get-tuple-element.42), channel_id=1, source_target_pairs={{0,1},{2,3},{4,5},{6,7},{8,9},{10,11},{12,13},{14,15},{16,17},{18,... | collective-permute-start | bytes 24584 | tf_op jit(solution)/shard_map/ppermute | solution.py:366
  19.0 4.1 %collective-permute-start.3 = (f32[16,128]{1,0:T(8,128)S(1)}, f32[16,128]{1,0:T(8,128)S(1)}, u32[]{:S(2)}, u32[]{:S(2)}) collective-permute-start(f32[16,128]{1,0:T(8,128)S(1)} %get-tuple-element.43), channel_id=1, source_target_pairs={{1,2},{5,6},{9,10},{13,14},{17,18},{21,22},{25,26},{29,30},{0,4},{... | collective-permute-start | bytes 24584 | tf_op jit(solution)/shard_map/ppermute | solution.py:366
  19.0 1.6 %collective-permute-start = (f32[3,128]{1,0:T(4,128)S(1)}, f32[3,128]{1,0:T(4,128)S(1)}, u32[]{:S(2)}, u32[]{:S(2)}) collective-permute-start(f32[3,128]{1,0:T(4,128)S(1)} %get-tuple-element.40), channel_id=1, source_target_pairs={{0,4},{1,5},{2,6},{3,7},{8,12},{9,13},{10,14},{11,15},{16,20},{17,... | collective-permute-start | bytes 4616 | tf_op jit(solution)/shard_map/ppermute | solution.py:366
  19.5 3.6 %collective-permute-start.1 = (f32[3,128]{1,0:T(4,128)S(1)}, f32[3,128]{1,0:T(4,128)S(1)}, u32[]{:S(2)}, u32[]{:S(2)}) collective-permute-start(f32[3,128]{1,0:T(4,128)S(1)} %get-tuple-element.41), channel_id=1, source_target_pairs={{4,8},{5,9},{6,10},{7,11},{12,16},{13,17},{14,18},{15,19},{20,24},... | collective-permute-start | bytes 4616 | tf_op jit(solution)/shard_map/ppermute | solution.py:366

commit v4 on v3

--- a/solution.py
+++ b/solution.py
@@ -104,7 +104,7 @@
 
 def project_kernel(
     leaf_t, node_t, values_hbm, basis_hbm, conduct_hbm,
-    sent_hbm, own, wide_high, wide_low, up_high, up_low, moves, values, conduct, basis, sent, sems,
+    sent_hbm, own, wide_high, wide_low, up_high, up_low, values, conduct, moves, basis, sent, sems,
 ):
     levels, rank = moves.shape[0], moves.shape[1]
     piece = basis.shape[0] // PIECES
@@ -155,21 +155,23 @@
 
 
 def window_kernel(
-    leaf_f, node_f, inverse_hbm, values, moves, up_high, up_low,
-    near, down_high, down_low, meet_high, meet_low, inverse, fronts, held, sems,
+    leaf_f, node_f, inverse_hbm, leaf_t, node_t, values, up_high, up_low,
+    near, down_high, down_low, meet_high, meet_low, inverse, moves, fronts, held, sems,
 ):
     levels, rank = moves.shape[0], moves.shape[1]
     copies = [
         pltpu.make_async_copy(leaf_f, fronts.at[0], sems.at[0]),
         pltpu.make_async_copy(node_f, fronts.at[pl.ds(1, levels)], sems.at[1]),
         pltpu.make_async_copy(inverse_hbm, inverse, sems.at[2]),
+        pltpu.make_async_copy(leaf_t, moves.at[0], sems.at[3]),
+        pltpu.make_async_copy(node_t, moves.at[pl.ds(1, moves.shape[0] - 1)], sems.at[4]),
     ]
-    for copy in copies:
-        copy.start()
+    for i in (0, 1, 3, 4, 2):
+        copies[i].start()
     columns = [slice(h * rank, (h + 1) * rank) for h in range(levels + 1)]
     back = [(up_high[:, at].astype(F32) + up_low[:, at].astype(F32)).T for at in columns[:levels]]
-    copies[0].wait()
-    copies[1].wait()
+    for i in (0, 1, 3, 4):
+        copies[i].wait()
     total = [fronts[0]] + [product(fronts[h + 1], back[h]) for h in range(levels)]
     for h in range(levels, -1, -1):
         if h == levels // 2:
@@ -183,6 +185,8 @@
             at = columns[h - 1]
             plain = up_high[:, at].astype(F32) + up_low[:, at].astype(F32)
             meet_high[:, at], meet_low[:, at] = parts(jnp.where(second, total[h].T, plain))
+        else:
+            meet_high[:, columns[levels]], meet_low[:, columns[levels]] = parts(total[0])
 
 
 def tree(got, own, down_high, down_low):
@@ -233,7 +237,7 @@
 
 
 def second_kernel(
-    x_inner, x_outer, y_inner, y_outer, z, conduct, wide_high, wide_low, meet_high, meet_low, down_high, down_low, inverse,
+    x_inner, x_outer, y_inner, y_outer, z, conduct, wide_high, wide_low, meet_high, meet_low, inverse,
     sums, applied, near, sent, home, held,
 ):
     count_s, extent_x, extent_y = z.shape
@@ -270,9 +274,9 @@
     leaf_map(applied, inverse, near, held)
     rank = coeffs.shape[1]
     chain = rows_times(coeffs, meet_high[...], meet_low[...])
-    back = rows_times(coeffs, down_high[0:rank, :], down_low[0:rank, :])
+    levels = chain.shape[1] // rank - 1
+    back = chain[:, levels * rank :]
     home[...] = back
-    levels = chain.shape[1] // rank
     for level in range(levels):
         row = chain[:, level * rank : (level + 1) * rank]
         sent[:, level] = jnp.broadcast_to(row[None], (sent.shape[0],) + row.shape)
@@ -316,7 +320,8 @@
         residual[s] = right[s] - steps[s : s + 1] * applied[s]
     copies[0].start()
     copies[1].start()
-    spread = home[...] + rows_times(jnp.concatenate(heard, axis=1), meet_high[...], meet_low[...], LANES)
+    rows = jnp.concatenate(heard, axis=1)
+    spread = home[...] + rows_times(rows, meet_high[:, : rows.shape[1]], meet_low[:, : rows.shape[1]], LANES)
     expand_into(mapped, spread, wide_high, wide_low, near)
     for s in range(count_s):
         direction[s] = z[s] - steps[s : s + 1] * mapped[s] + ratios[s : s + 1] * z[s]
@@ -411,20 +416,20 @@
     def pair(*shape):
         return (in_vmem(*shape, dtype=BF16),) * 2
 
-    sent, own, wide_high, wide_low, up_high, up_low, moves, right_side, conductivity = call(
+    sent, own, wide_high, wide_low, up_high, up_low, right_side, conductivity = call(
         project_kernel,
         (
             in_hbm(count, count_s, rank),
             in_vmem(count_s, rank),
             *pair(rank, cells),
             *pair(rank, levels * rank),
-            in_vmem(levels, rank, rank),
             in_vmem(*field),
             in_vmem(extent_x, extent_y),
         ),
         (),
         10**6,
         (
+            pltpu.VMEM((levels, rank, rank), F32),
             pltpu.VMEM((cells, rank), F32),
             pltpu.VMEM((count, count_s, rank), F32),
             pltpu.SemaphoreType.DMA((5 + PIECES,)),
@@ -439,13 +444,18 @@
         (
             in_vmem(*field),
             *pair((levels + 1) * rank, rank),
-            *pair(rank, levels * rank),
+            *pair(rank, (levels + 1) * rank),
             in_vmem(*leaf_inverse.shape),
         ),
-        (right_side, moves, up_high, up_low),
+        (right_side, up_high, up_low),
         10**7,
-        (pltpu.VMEM((levels + 1, rank, rank), F32), held, pltpu.SemaphoreType.DMA((3,))),
-        (leaf_f, node_f, leaf_inverse),
+        (
+            pltpu.VMEM((levels, rank, rank), F32),
+            pltpu.VMEM((levels + 1, rank, rank), F32),
+            held,
+            pltpu.SemaphoreType.DMA((5,)),
+        ),
+        (leaf_f, node_f, leaf_inverse, leaf_t, node_t),
     )
     edge = (count_s + 1, extent_y)
     first_z, x_inner, x_outer, y_inner, y_outer, sums = call(
@@ -467,7 +477,7 @@
         ),
         (
             x_inner, x_outer, y_inner, y_outer, first_z, conductivity,
-            wide_high, wide_low, meet_high, meet_low, down_high, down_low, inverse, sums,
+            wide_high, wide_low, meet_high, meet_low, inverse, sums,
         ),
         10**6,
         (held,),

time: 38.2 us -> 38.2 us (level)
  no operation moved by 1% of the time
where the time goes in v4:
time: 38.2 us; the launch traced here: 38 us
  blocking collectives  12.5 us (33%)
  starting transfers between devices  9.43 us (25%)
  Pallas kernels  8.33 us (22%)
  waiting for transfers between devices  6.98 us (18%)
  between operations  0.67 us (2%)
    all_to_all x1, blocking collectives, on_device(): got = lax.all_to_all(sent, AXES, 0, 0)  12.5 us
    pallas_call x5, Pallas kernels, call(): pl.pallas_call(body, out_shape=tuple(outs), in_specs=[hbm] * len(fetched)...  8.33 us
    all_to_all x1, starting transfers between devices, on_device(): got = lax.all_to_all(sent, AXES, 0, 0)  7.33 us
    all_to_all x1, waiting for transfers between devices, on_device(): got = lax.all_to_all(sent, AXES, 0, 0)  4.51 us
    ppermute x4, waiting for transfers between devices, swap(): return lax.ppermute(value, AXES, pairs + [(j, i) for i, j in pairs])  2.47 us
    ppermute x4, starting transfers between devices, swap(): return lax.ppermute(value, AXES, pairs + [(j, i) for i, j in pairs])  2.1 us
  transfers between devices with their start and end apart: 5, of which 2 were waited for; matrix products, arithmetic and copies ran while one was open for 0% of the time, Pallas kernels for 7%

profile of v4, /device:TPU:0, one launch (start us, length us, event | category | flops | bytes accessed | tf_op | source)
XLA Modules:
  0.0 38.0 jit_solution(18329200022320285147)
XLA Ops:
  0.6 2.6 %shard_map.103 = (f32[32,2,128]{2,1,0:T(2,128)}, f32[2,128]{1,0:T(2,128)S(1)}, bf16[128,2048]{1,0:T(8,128)(2,1)S(1)}, bf16[128,2048]{1,0:T(8,128)(2,1)S(1)}, bf1...) custom-call(f32[128,128]{1,0:T(8,128)} %bitcast.9, ...), custom_call_target="tpu_custom_call" | custom-call | flops 1000000 | tf_op jit(solution)/shard_map/pallas_call | solution.py:63
  3.3 7.3 %all-to-all-start = ((f32[32,2,128]{2,1,0:T(2,128)}), f32[32,2,128]{2,1,0:T(2,128)S(1)}, u32[]{:S(2)}, u32[]{:S(2)}) async-start(f32[32,2,128]{2,1,0:T(2,128)} %get-tuple-element.27), calls=%async_computation | async-start | bytes 65536 | tf_op jit(solution)/shard_map/all_to_all | solution.py:440
  10.6 2.8 %shard_map.104 = (f32[2,16,128]{2,1,0:T(8,128)S(1)}, bf16[768,128]{1,0:T(8,128)(2,1)S(1)}, bf16[768,128]{1,0:T(8,128)(2,1)S(1)}, bf16[128,768]{1,0:T(8,128)(2,1)...) custom-call(f32[128,128]{1,0:T(8,128)} %bitcast.11, f32[5,128,128]{2,1,0:T(8,128)} %bitcast.8, ...), custom_call_target="tpu_custom_call" | custom-call | flops 10000000 | bytes 344064 | tf_op jit(solution)/shard_map/pallas_call | solution.py:63
  13.4 4.5 %all-to-all-done.got = f32[32,2,128]{2,1,0:T(2,128)S(1)} async-done(((f32[32,2,128]{2,1,0:T(2,128)}), f32[32,2,128]{2,1,0:T(2,128)S(1)}, u32[]{:S(2)}, u32[]{:S(2)}) %all-to-all-start) | async-done | bytes 32800 | tf_op jit(solution)/shard_map/all_to_all | solution.py:440
  17.9 0.6 %shard_map.105 = (f32[2,16,128]{2,1,0:T(8,128)S(1)}, f32[3,128]{1,0:T(4,128)S(1)}, f32[3,128]{1,0:T(4,128)S(1)}, f32[16,128]{1,0:T(8,128)S(1)}, f32[16,128]{1,0:T(8,128)S(1)}, /*index=5*/f32[2,128]{1,0:T(2,128)S(1)}) custom-call(f32[32,2,128]{2,1,0:T(2,128)S(1)} %all-to-all-done.got, f32[2,128]{1,0:T(2,128)S(1)} %get-tuple-element.28.own, ...), custom_call_target="tpu_custom_call" | custom-call | flops 1000000 | bytes 1516544 | tf_op jit(solution)/shard_map/pallas_call | solution.py:63
  18.5 0.5 %collective-permute-start.2 = (f32[16,128]{1,0:T(8,128)S(1)}, f32[16,128]{1,0:T(8,128)S(1)}, u32[]{:S(2)}, u32[]{:S(2)}) collective-permute-start(f32[16,128]{1,0:T(8,128)S(1)} %get-tuple-element.40), channel_id=1, source_target_pairs={{0,1},{2,3},{4,5},{6,7},{8,9},{10,11},{12,13},{14,15},{16,17},{18,... | collective-permute-start | bytes 24584 | tf_op jit(solution)/shard_map/ppermute | solution.py:371
  19.0 0.0 collective-permute-start.3
  19.0 0.5 %collective-permute-start = (f32[3,128]{1,0:T(4,128)S(1)}, f32[3,128]{1,0:T(4,128)S(1)}, u32[]{:S(2)}, u32[]{:S(2)}) collective-permute-start(f32[3,128]{1,0:T(4,128)S(1)} %get-tuple-element.38), channel_id=1, source_target_pairs={{0,4},{1,5},{2,6},{3,7},{8,12},{9,13},{10,14},{11,15},{16,20},{17,... | collective-permute-start | bytes 4616 | tf_op jit(solution)/shard_map/ppermute | solution.py:371
  19.5 1.1 %collective-permute-start.1 = (f32[3,128]{1,0:T(4,128)S(1)}, f32[3,128]{1,0:T(4,128)S(1)}, u32[]{:S(2)}, u32[]{:S(2)}) collective-permute-start(f32[3,128]{1,0:T(4,128)S(1)} %get-tuple-element.39), channel_id=1, source_target_pairs={{4,8},{5,9},{6,10},{7,11},{12,16},{13,17},{14,18},{15,19},{20,24},... | collective-permute-start | bytes 4616 | tf_op jit(solution)/shard_map/ppermute | solution.py:371
  20.6 0.0 collective-permute-done.x_inner
  20.6 2.5 %collective-permute-done.1.x_outer = f32[3,128]{1,0:T(4,128)S(1)} collective-permute-done((f32[3,128]{1,0:T(4,128)S(1)}, f32[3,128]{1,0:T(4,128)S(1)}, u32[]{:S(2)}, u32[]{:S(2)}) %collective-permute-start.1) | collective-permute-done | bytes 1568 | tf_op jit(solution)/shard_map/ppermute | solution.py:371
  23.0 0.0 collective-permute-done.2.y_inner
  23.1 0.0 collective-permute-done.3.y_outer
  23.1 1.0 %shard_map.106 = (f32[2,16,128]{2,1,0:T(8,128)S(1)}, f32[2,16,128]{2,1,0:T(8,128)S(1)}, f32[32,6,2,128]{3,2,1,0:T(2,128)S(1)}, f32[2,128]{1,0:T(2,128)S(1)}) custom-call(f32[3,128]{1,0:T(4,128)S(1)} %collective-permute-done.x_inner, f32[3,128]{1,0:T(4,128)S(1)} %collective-permute-done.1.x_outer, f32[16,128]{1,0:T(8,128)S(1)} %collective-permute-done.2.y_inner, ...), custom_call_target="tpu_custom_call" | custom-call | flops 1000000 | bytes 2535424 | tf_op jit(solution)/shard_map/pallas_call | solution.py:63
  24.1 12.5 %all_to_all.10.got = f32[32,6,2,128]{3,2,1,0:T(2,128)S(1)} all-to-all(f32[32,6,2,128]{3,2,1,0:T(2,128)S(1)} %get-tuple-element.47), channel_id=1, replica_groups=mesh['gx'=8,'gy'=4] {'gx','gy'}, dimensions={0} | all-to-all | bytes 393216 | tf_op jit(solution)/shard_map/all_to_all | solution.py:485
  36.6 1.3 %shard_map.107 = (f32[2,16,128]{2,1,0:T(8,128)}, f32[2,16,128]{2,1,0:T(8,128)}, f32[2,16,128]{2,1,0:T(8,128)}) custom-call(f32[32,6,2,128]{3,2,1,0:T(2,128)S(1)} %all_to_all.10.got, f32[2,128]{1,0:T(2,128)S(1)} %get-tuple-element.48.home, bf16[128,768]{1,0:T(8,128)(2,1)S(1)} %get-tuple-element.43.meet_high, bf16[128,768]{1,0:T(8,128)(2,1)S(1)} %get-tuple-element.44.meet_low, ...), custom_call_target="tpu_custom_call" | custom-call | flops 1000000 | bytes 1704960 | tf_op jit(solution)/shard_map/pallas_call | solution.py:63
Async XLA Ops:
  3.3 14.6 %all-to-all-start = ((f32[32,2,128]{2,1,0:T(2,128)}), f32[32,2,128]{2,1,0:T(2,128)S(1)}, u32[]{:S(2)}, u32[]{:S(2)}) async-start(f32[32,2,128]{2,1,0:T(2,128)} %get-tuple-element.27), calls=%async_computation | async-start | bytes 65536 | tf_op jit(solution)/shard_map/all_to_all | solution.py:440
  18.5 4.6 %collective-permute-start.2 = (f32[16,128]{1,0:T(8,128)S(1)}, f32[16,128]{1,0:T(8,128)S(1)}, u32[]{:S(2)}, u32[]{:S(2)}) collective-permute-start(f32[16,128]{1,0:T(8,128)S(1)} %get-tuple-element.40), channel_id=1, source_target_pairs={{0,1},{2,3},{4,5},{6,7},{8,9},{10,11},{12,13},{14,15},{16,17},{18,... | collective-permute-start | bytes 24584 | tf_op jit(solution)/shard_map/ppermute | solution.py:371
  19.0 4.1 %collective-permute-start.3 = (f32[16,128]{1,0:T(8,128)S(1)}, f32[16,128]{1,0:T(8,128)S(1)}, u32[]{:S(2)}, u32[]{:S(2)}) collective-permute-start(f32[16,128]{1,0:T(8,128)S(1)} %get-tuple-element.41), channel_id=1, source_target_pairs={{1,2},{5,6},{9,10},{13,14},{17,18},{21,22},{25,26},{29,30},{0,4},{... | collective-permute-start | bytes 24584 | tf_op jit(solution)/shard_map/ppermute | solution.py:371
  19.0 1.6 %collective-permute-start = (f32[3,128]{1,0:T(4,128)S(1)}, f32[3,128]{1,0:T(4,128)S(1)}, u32[]{:S(2)}, u32[]{:S(2)}) collective-permute-start(f32[3,128]{1,0:T(4,128)S(1)} %get-tuple-element.38), channel_id=1, source_target_pairs={{0,4},{1,5},{2,6},{3,7},{8,12},{9,13},{10,14},{11,15},{16,20},{17,... | collective-permute-start | bytes 4616 | tf_op jit(solution)/shard_map/ppermute | solution.py:371
  19.5 3.6 %collective-permute-start.1 = (f32[3,128]{1,0:T(4,128)S(1)}, f32[3,128]{1,0:T(4,128)S(1)}, u32[]{:S(2)}, u32[]{:S(2)}) collective-permute-start(f32[3,128]{1,0:T(4,128)S(1)} %get-tuple-element.39), channel_id=1, source_target_pairs={{4,8},{5,9},{6,10},{7,11},{12,16},{13,17},{14,18},{15,19},{20,24},... | collective-permute-start | bytes 4616 | tf_op jit(solution)/shard_map/ppermute | solution.py:371

commit v5 on v4

--- a/solution.py
+++ b/solution.py
@@ -298,8 +298,10 @@
     copies = [
         pltpu.make_async_copy(solution, solution_hbm, sems.at[0]),
         pltpu.make_async_copy(residual, residual_hbm, sems.at[1]),
-        pltpu.make_async_copy(direction, direction_hbm, sems.at[2]),
     ]
+    for part in range(2):
+        at = pl.ds(part * (direction.shape[1] // 2), direction.shape[1] // 2)
+        copies.append(pltpu.make_async_copy(direction.at[:, at], direction_hbm.at[:, at], sems.at[2 + part]))
     heard, cross = [], jnp.zeros(home.shape, F32)
     for level in range(1, levels + 1):
         size = 1 << (level - 1)
@@ -322,10 +324,19 @@
     copies[1].start()
     rows = jnp.concatenate(heard, axis=1)
     spread = home[...] + rows_times(rows, meet_high[:, : rows.shape[1]], meet_low[:, : rows.shape[1]], LANES)
-    expand_into(mapped, spread, wide_high, wide_low, near)
-    for s in range(count_s):
-        direction[s] = z[s] - steps[s : s + 1] * mapped[s] + ratios[s : s + 1] * z[s]
-    copies[2].start()
+    extent_x, width = direction.shape[1], direction.shape[2]
+    half = extent_x // 2
+    for part in range(2):
+        rows = slice(part * half, (part + 1) * half)
+        cells = slice(part * half * width, (part + 1) * half * width)
+        far = rows_times(spread, wide_high[:, cells], wide_low[:, cells])
+        for x in range(half):
+            at = part * half + x
+            mapped[:, at, :] = near[:, at, :] + far[:, x * width : (x + 1) * width]
+        for s in range(count_s):
+            rest = z[s, rows, :] - steps[s : s + 1] * mapped[s, rows, :]
+            direction[s, rows, :] = rest + ratios[s : s + 1] * z[s, rows, :]
+        copies[2 + part].start()
     for copy in copies:
         copy.wait()
 
@@ -488,7 +499,7 @@
         (in_hbm(*field),) * 3,
         (got, home, meet_high, meet_low, wide_high, wide_low, near, first_z, right_side, applied),
         10**6,
-        (pltpu.VMEM(field, F32),) * 4 + (pltpu.SemaphoreType.DMA((3,)),),
+        (pltpu.VMEM(field, F32),) * 4 + (pltpu.SemaphoreType.DMA((4,)),),
         written=3,
     )
 

time: 38.2 us -> 38.2 us (level)
  no operation moved by 1% of the time
where the time goes in v5:
time: 38.2 us; the launch traced here: 38 us
  blocking collectives  12.5 us (33%)
  starting transfers between devices  9.43 us (25%)
  Pallas kernels  8.34 us (22%)
  waiting for transfers between devices  6.98 us (18%)
  between operations  0.67 us (2%)
    all_to_all x1, blocking collectives, on_device(): got = lax.all_to_all(sent, AXES, 0, 0)  12.5 us
    pallas_call x5, Pallas kernels, call(): pl.pallas_call(body, out_shape=tuple(outs), in_specs=[hbm] * len(fetched)...  8.34 us
    all_to_all x1, starting transfers between devices, on_device(): got = lax.all_to_all(sent, AXES, 0, 0)  7.33 us
    all_to_all x1, waiting for transfers between devices, on_device(): got = lax.all_to_all(sent, AXES, 0, 0)  4.51 us
    ppermute x4, waiting for transfers between devices, swap(): return lax.ppermute(value, AXES, pairs + [(j, i) for i, j in pairs])  2.47 us
    ppermute x4, starting transfers between devices, swap(): return lax.ppermute(value, AXES, pairs + [(j, i) for i, j in pairs])  2.1 us
  transfers between devices with their start and end apart: 5, of which 2 were waited for; matrix products, arithmetic and copies ran while one was open for 0% of the time, Pallas kernels for 7%

profile of v5, /device:TPU:0, one launch (start us, length us, event | category | flops | bytes accessed | tf_op | source)
XLA Modules:
  0.0 38.0 jit_solution(14800068403713867897)
XLA Ops:
  0.6 2.6 %shard_map.103 = (f32[32,2,128]{2,1,0:T(2,128)}, f32[2,128]{1,0:T(2,128)S(1)}, bf16[128,2048]{1,0:T(8,128)(2,1)S(1)}, bf16[128,2048]{1,0:T(8,128)(2,1)S(1)}, bf1...) custom-call(f32[128,128]{1,0:T(8,128)} %bitcast.9, ...), custom_call_target="tpu_custom_call" | custom-call | flops 1000000 | tf_op jit(solution)/shard_map/pallas_call | solution.py:63
  3.3 7.3 %all-to-all-start = ((f32[32,2,128]{2,1,0:T(2,128)}), f32[32,2,128]{2,1,0:T(2,128)S(1)}, u32[]{:S(2)}, u32[]{:S(2)}) async-start(f32[32,2,128]{2,1,0:T(2,128)} %get-tuple-element.27), calls=%async_computation | async-start | bytes 65536 | tf_op jit(solution)/shard_map/all_to_all | solution.py:451
  10.6 2.8 %shard_map.104 = (f32[2,16,128]{2,1,0:T(8,128)S(1)}, bf16[768,128]{1,0:T(8,128)(2,1)S(1)}, bf16[768,128]{1,0:T(8,128)(2,1)S(1)}, bf16[128,768]{1,0:T(8,128)(2,1)...) custom-call(f32[128,128]{1,0:T(8,128)} %bitcast.11, f32[5,128,128]{2,1,0:T(8,128)} %bitcast.8, ...), custom_call_target="tpu_custom_call" | custom-call | flops 10000000 | bytes 344064 | tf_op jit(solution)/shard_map/pallas_call | solution.py:63
  13.4 4.5 %all-to-all-done.got = f32[32,2,128]{2,1,0:T(2,128)S(1)} async-done(((f32[32,2,128]{2,1,0:T(2,128)}), f32[32,2,128]{2,1,0:T(2,128)S(1)}, u32[]{:S(2)}, u32[]{:S(2)}) %all-to-all-start) | async-done | bytes 32800 | tf_op jit(solution)/shard_map/all_to_all | solution.py:451
  17.9 0.6 %shard_map.105 = (f32[2,16,128]{2,1,0:T(8,128)S(1)}, f32[3,128]{1,0:T(4,128)S(1)}, f32[3,128]{1,0:T(4,128)S(1)}, f32[16,128]{1,0:T(8,128)S(1)}, f32[16,128]{1,0:T(8,128)S(1)}, /*index=5*/f32[2,128]{1,0:T(2,128)S(1)}) custom-call(f32[32,2,128]{2,1,0:T(2,128)S(1)} %all-to-all-done.got, f32[2,128]{1,0:T(2,128)S(1)} %get-tuple-element.28.own, ...), custom_call_target="tpu_custom_call" | custom-call | flops 1000000 | bytes 1516544 | tf_op jit(solution)/shard_map/pallas_call | solution.py:63
  18.5 0.5 %collective-permute-start.2 = (f32[16,128]{1,0:T(8,128)S(1)}, f32[16,128]{1,0:T(8,128)S(1)}, u32[]{:S(2)}, u32[]{:S(2)}) collective-permute-start(f32[16,128]{1,0:T(8,128)S(1)} %get-tuple-element.40), channel_id=1, source_target_pairs={{0,1},{2,3},{4,5},{6,7},{8,9},{10,11},{12,13},{14,15},{16,17},{18,... | collective-permute-start | bytes 24584 | tf_op jit(solution)/shard_map/ppermute | solution.py:382
  19.0 0.0 collective-permute-start.3
  19.0 0.5 %collective-permute-start = (f32[3,128]{1,0:T(4,128)S(1)}, f32[3,128]{1,0:T(4,128)S(1)}, u32[]{:S(2)}, u32[]{:S(2)}) collective-permute-start(f32[3,128]{1,0:T(4,128)S(1)} %get-tuple-element.38), channel_id=1, source_target_pairs={{0,4},{1,5},{2,6},{3,7},{8,12},{9,13},{10,14},{11,15},{16,20},{17,... | collective-permute-start | bytes 4616 | tf_op jit(solution)/shard_map/ppermute | solution.py:382
  19.5 1.1 %collective-permute-start.1 = (f32[3,128]{1,0:T(4,128)S(1)}, f32[3,128]{1,0:T(4,128)S(1)}, u32[]{:S(2)}, u32[]{:S(2)}) collective-permute-start(f32[3,128]{1,0:T(4,128)S(1)} %get-tuple-element.39), channel_id=1, source_target_pairs={{4,8},{5,9},{6,10},{7,11},{12,16},{13,17},{14,18},{15,19},{20,24},... | collective-permute-start | bytes 4616 | tf_op jit(solution)/shard_map/ppermute | solution.py:382
  20.6 0.0 collective-permute-done.x_inner
  20.6 2.5 %collective-permute-done.1.x_outer = f32[3,128]{1,0:T(4,128)S(1)} collective-permute-done((f32[3,128]{1,0:T(4,128)S(1)}, f32[3,128]{1,0:T(4,128)S(1)}, u32[]{:S(2)}, u32[]{:S(2)}) %collective-permute-start.1) | collective-permute-done | bytes 1568 | tf_op jit(solution)/shard_map/ppermute | solution.py:382
  23.0 0.0 collective-permute-done.2.y_inner
  23.1 0.0 collective-permute-done.3.y_outer
  23.1 1.0 %shard_map.106 = (f32[2,16,128]{2,1,0:T(8,128)S(1)}, f32[2,16,128]{2,1,0:T(8,128)S(1)}, f32[32,6,2,128]{3,2,1,0:T(2,128)S(1)}, f32[2,128]{1,0:T(2,128)S(1)}) custom-call(f32[3,128]{1,0:T(4,128)S(1)} %collective-permute-done.x_inner, f32[3,128]{1,0:T(4,128)S(1)} %collective-permute-done.1.x_outer, f32[16,128]{1,0:T(8,128)S(1)} %collective-permute-done.2.y_inner, ...), custom_call_target="tpu_custom_call" | custom-call | flops 1000000 | bytes 2535424 | tf_op jit(solution)/shard_map/pallas_call | solution.py:63
  24.1 12.5 %all_to_all.10.got = f32[32,6,2,128]{3,2,1,0:T(2,128)S(1)} all-to-all(f32[32,6,2,128]{3,2,1,0:T(2,128)S(1)} %get-tuple-element.47), channel_id=1, replica_groups=mesh['gx'=8,'gy'=4] {'gx','gy'}, dimensions={0} | all-to-all | bytes 393216 | tf_op jit(solution)/shard_map/all_to_all | solution.py:496
  36.6 1.3 %shard_map.107 = (f32[2,16,128]{2,1,0:T(8,128)}, f32[2,16,128]{2,1,0:T(8,128)}, f32[2,16,128]{2,1,0:T(8,128)}) custom-call(f32[32,6,2,128]{3,2,1,0:T(2,128)S(1)} %all_to_all.10.got, f32[2,128]{1,0:T(2,128)S(1)} %get-tuple-element.48.home, bf16[128,768]{1,0:T(8,128)(2,1)S(1)} %get-tuple-element.43.meet_high, bf16[128,768]{1,0:T(8,128)(2,1)S(1)} %get-tuple-element.44.meet_low, ...), custom_call_target="tpu_custom_call" | custom-call | flops 1000000 | bytes 1704960 | tf_op jit(solution)/shard_map/pallas_call | solution.py:63
Async XLA Ops:
  3.3 14.6 %all-to-all-start = ((f32[32,2,128]{2,1,0:T(2,128)}), f32[32,2,128]{2,1,0:T(2,128)S(1)}, u32[]{:S(2)}, u32[]{:S(2)}) async-start(f32[32,2,128]{2,1,0:T(2,128)} %get-tuple-element.27), calls=%async_computation | async-start | bytes 65536 | tf_op jit(solution)/shard_map/all_to_all | solution.py:451
  18.5 4.6 %collective-permute-start.2 = (f32[16,128]{1,0:T(8,128)S(1)}, f32[16,128]{1,0:T(8,128)S(1)}, u32[]{:S(2)}, u32[]{:S(2)}) collective-permute-start(f32[16,128]{1,0:T(8,128)S(1)} %get-tuple-element.40), channel_id=1, source_target_pairs={{0,1},{2,3},{4,5},{6,7},{8,9},{10,11},{12,13},{14,15},{16,17},{18,... | collective-permute-start | bytes 24584 | tf_op jit(solution)/shard_map/ppermute | solution.py:382
  19.0 4.1 %collective-permute-start.3 = (f32[16,128]{1,0:T(8,128)S(1)}, f32[16,128]{1,0:T(8,128)S(1)}, u32[]{:S(2)}, u32[]{:S(2)}) collective-permute-start(f32[16,128]{1,0:T(8,128)S(1)} %get-tuple-element.41), channel_id=1, source_target_pairs={{1,2},{5,6},{9,10},{13,14},{17,18},{21,22},{25,26},{29,30},{0,4},{... | collective-permute-start | bytes 24584 | tf_op jit(solution)/shard_map/ppermute | solution.py:382
  19.0 1.6 %collective-permute-start = (f32[3,128]{1,0:T(4,128)S(1)}, f32[3,128]{1,0:T(4,128)S(1)}, u32[]{:S(2)}, u32[]{:S(2)}) collective-permute-start(f32[3,128]{1,0:T(4,128)S(1)} %get-tuple-element.38), channel_id=1, source_target_pairs={{0,4},{1,5},{2,6},{3,7},{8,12},{9,13},{10,14},{11,15},{16,20},{17,... | collective-permute-start | bytes 4616 | tf_op jit(solution)/shard_map/ppermute | solution.py:382
  19.5 3.6 %collective-permute-start.1 = (f32[3,128]{1,0:T(4,128)S(1)}, f32[3,128]{1,0:T(4,128)S(1)}, u32[]{:S(2)}, u32[]{:S(2)}) collective-permute-start(f32[3,128]{1,0:T(4,128)S(1)} %get-tuple-element.39), channel_id=1, source_target_pairs={{4,8},{5,9},{6,10},{7,11},{12,16},{13,17},{14,18},{15,19},{20,24},... | collective-permute-start | bytes 4616 | tf_op jit(solution)/shard_map/ppermute | solution.py:382
